TPU v7x, 128 devices: a whole 4x4x4 slice. The times are simulated.
128 devices in a mesh: inp: 8 (over z, x_hi), tm: 8 (over x_lo, y), bl: 2 (over core).
Axes of the slice: x: 4 (x_hi: 2, x_lo: 2; x = x_hi * 2 + x_lo), y: 4, z: 4, core: 2. Of those that a mesh axis runs over, the one named last changes fastest.
Arguments:
- voltages: int32 [1024, 524288], P(('inp', 'bl'), 'tm'), may hold values from -16 to 14, as said below
- taps: float32 [4, 16384], replicated, may hold values from -3 to 3
- flags: int32 [1024], P(('inp', 'bl')), may hold values 0 or 1
Outputs:
- visibilities: float32 [2, 128, 8, 128, 1024], P(None, ('inp', 'tm'), None, 'bl')
Inputs may be any that keep to these rules, and one draw needn't show every extreme that they name: `voltages`: int8-valued digitized samples, each input's stream in time order.
All inputs are finite; a program needn't handle non-finite values. No bound on the sum of `flags` on one device may be relied on, other than what follows from the above.
Results may differ from a plain program's by a relative error of at most 0.00065.
Values may be sent and summed in bfloat16 or wider, within the bound.
A program may use at most 192 MiB of HBM per device.

v0:
```python
import math

import jax
import jax.numpy as jnp
from jax import lax
from jax.sharding import PartitionSpec as P

CH_AVG = 64


def passed_along(value, axis, steps):
    count = lax.axis_size(axis)
    initial, last = (max(0, -steps), min(count, count - steps))
    return lax.ppermute(value, axis, [(source, source + steps) for source in range(initial, last)])


def cos_sin(height, breadth, period):
    grid = lax.broadcasted_iota(jnp.int32, (height, breadth), 0) * lax.broadcasted_iota(
        jnp.int32, (height, breadth), 1
    )
    angle = (grid % period).astype(jnp.float32) * (2.0 * math.pi / period)
    return (jnp.cos(angle), jnp.sin(angle))


def transform(filtered, length):
    batch = filtered.shape[0]
    first_len = 128
    second_len = length // first_len
    highest = lax.Precision.HIGHEST
    blocks = filtered.reshape(batch, first_len, second_len)
    cos_one, sin_one = cos_sin(first_len, first_len, first_len)
    table_one = jnp.stack([cos_one, -sin_one])
    section_one = jnp.einsum("ykn,mnb->mykb", table_one, blocks, precision=highest)
    cos_twist, sin_twist = cos_sin(first_len, second_len, length)
    real_one = section_one[:, 0]
    imag_one = section_one[:, 1]
    twisted = jnp.stack(
        [real_one * cos_twist + imag_one * sin_twist, imag_one * cos_twist - real_one * sin_twist],
        axis=1,
    )
    cos_two, sin_two = cos_sin(second_len, second_len // 2, second_len)
    table_two = jnp.stack(
        [jnp.stack([cos_two, -sin_two], axis=1), jnp.stack([sin_two, cos_two], axis=1)]
    )
    result = jnp.einsum("mxkb,xbyq->ymqk", twisted, table_two, precision=highest)
    return result.reshape(2, batch, length // 2)


def shards(voltages, taps, flags):
    inputs = voltages.shape[0]
    tap_count = taps.shape[0]
    length = taps.shape[1]
    spectra_dev = voltages.shape[1] // length
    reach = tap_count - 1
    samples = voltages.astype(jnp.float32).reshape(inputs, spectra_dev, length)
    leading = voltages[:, : reach * length].reshape(inputs, reach, length).astype(jnp.bfloat16)
    following = passed_along(leading, "tm", -1)
    extended = jnp.concatenate([samples, following.astype(jnp.float32)], axis=1)
    filtered = jnp.zeros((inputs, spectra_dev, length), jnp.float32)
    for offset in range(tap_count):
        filtered = (
            filtered + taps[offset][None, None, :] * extended[:, offset : offset + spectra_dev]
        )
    channels = length // 2
    both_parts = transform(filtered.reshape(inputs * spectra_dev, length), length)
    scale = flags.astype(jnp.float32)[None, :, None, None] / (8.0 * math.sqrt(length))
    spectra = (both_parts.reshape(2, inputs, spectra_dev, channels) * scale).astype(jnp.bfloat16)
    turned = lax.all_to_all(
        spectra[:, None], ("inp", "tm"), split_axis=4, concat_axis=1, tiled=True
    )
    groups_inp = lax.axis_size("inp")
    groups_tm = lax.axis_size("tm")
    local_channels = channels // (groups_inp * groups_tm)
    out_groups = local_channels // CH_AVG
    rows = turned.reshape(2, groups_inp, groups_tm, inputs, spectra_dev, out_groups, CH_AVG)
    count = float(groups_tm * spectra_dev * CH_AVG)
    products = jnp.einsum(
        "xatisgk,yctjsgk->gxyaicj",
        rows,
        lax.all_gather(rows, "bl", axis=3, tiled=True),
        preferred_element_type=jnp.float32,
    )
    real_vis = products[:, 0, 0] + products[:, 1, 1]
    imag_vis = products[:, 1, 0] - products[:, 0, 1]
    visibilities = jnp.stack([real_vis, imag_vis]) / count
    return visibilities.reshape(
        2, out_groups, groups_inp, inputs, groups_inp * inputs * lax.axis_size("bl")
    )


def solution(mesh):
    in_specs = (P(("inp", "bl"), "tm"), P(), P(("inp", "bl")))
    out_specs = P(None, ("inp", "tm"), None, "bl", None)
    return jax.shard_map(shards, mesh=mesh, in_specs=in_specs, out_specs=out_specs, check_vma=False)
```

profile of v0, /device:TPU:1, one launch (start us, length us, event | category | flops | bytes accessed | tf_op | source)
XLA Modules:
  0.0 725.3 jit_solution(16236080894492939012)
XLA Ops:
  6.5 5.2 slice_convert_fusion
  11.8 3.1 copy.89
  14.9 1.3 collective-permute-start
  16.2 11.3 %convert_element_type.80 = f32[64,65536]{1,0:T(8,128)} convert(s32[64,65536]{1,0:T(8,128)} %param.3) | non-fusion elementwise | flops 4194304 | bytes 33554432 | tf_op jit(solution)/shard_map/convert_element_type | solution.py:55
  27.5 17.6 %reshape.218 = f32[64,4,16384]{2,1,0:T(4,128)} reshape(f32[64,65536]{1,0:T(8,128)} %convert_element_type.80) | data formatting | bytes 33554432 | tf_op jit(solution)/shard_map/reshape | solution.py:55
  45.4 0.3 sine_negate_fusion
  45.6 0.3 fusion.45
  46.0 0.2 fusion.56
  46.2 107.9 %collective-permute-done = bf16[64,3,16384]{2,0,1:T(8,128)(2,1)} collective-permute-done((bf16[64,3,16384]{2,0,1:T(8,128)(2,1)}, bf16[64,3,16384]{2,0,1:T(8,128)(2,1)}, u32[]{:S(2)}, u32[]{:S(2)}) %collective-permute-start) | collective-permute-done | bytes 6291488 | tf_op jit(solution)/shard_map/ppermute | solution.py:14
  154.1 11.2 %copy.53 = f32[64,3,16384]{2,1,0:T(4,128)} copy(bf16[64,3,16384]{2,0,1:T(8,128)(2,1)} %collective-permute-done) | data formatting | bytes 18874368 | tf_op jit(solution)/shard_map/convert_element_type | solution.py:58
  165.3 32.6 %fusion.8 = f32[64,4,16384]{2,1,0:T(4,128)} fusion(f32[64,4,16384]{2,1,0:T(4,128)S(1)} %copy-done, f32[64,3,16384]{2,1,0:T(4,128)} %copy.53, f32[16384]{0:T(1024)S(1)} %bitcast.77, f32[16384]{0:T(1024)S(1)} %bitcast.78, f32[16384]{0:T(1024)S(1)} %bitcast.76, f32[16384]{0:T(1024)S(1)} %bitcast.75), kind=kLoop, calls=%fused_computation.13 | loop fusion | flops 41943040 | bytes 46399488 | tf_op jit(solution)/shard_map/add | solution.py:62
  197.9 20.5 %reshape_reshape.6 = f32[256,128,128]{2,1,0:T(8,128)} reshape(f32[64,4,16384]{2,1,0:T(4,128)} %fusion.8) | data formatting | bytes 33554432 | tf_op jit(solution)/shard_map/reshape;reshape | solution.py:30
  218.4 32.5 %fusion.17 = f32[256,2,128,128]{2,3,1,0:T(8,128)} fusion(f32[256,128,128]{2,1,0:T(8,128)} %reshape_reshape.6, f32[1,128,128]{2,1,0:T(8,128)S(1)} %get-tuple-element.15, f32[1,128,128]{2,1,0:T(8,128)S(1)} %get-tuple-element.16), kind=kOutput, calls=%fused_computation.26 | convolution fusion | flops 12884934656 | bytes 50462720 | tf_op jit(solution)/shard_map/ykn,mnb->mykb/dot_general | solution.py:33
  250.8 17.8 %multiply_add_fusion = (f32[256,1,128,128]{2,3,1,0:T(8,128)S(1)}, f32[256,1,128,128]{2,3,1,0:T(8,128)}) fusion(f32[256,2,128,128]{2,3,1,0:T(8,128)} %fusion.17, f32[128,128]{0,1:T(8,128)S(1)} %get-tuple-element.17, f32[128,128]{0,1:T(8,128)S(1)} %get-tuple-element.18), kind=kLoop, calls=%fused_computation.25 | loop fusion | flops 25165824 | bytes 67239936 | tf_op jit(solution)/shard_map/add | solution.py:38
  268.6 23.6 %fusion.25 = f32[2,256,64,128]{3,2,1,0:T(8,128)} fusion(f32[256,1,128,128]{2,3,1,0:T(8,128)} %get-tuple-element.6, f32[256,1,128,128]{2,3,1,0:T(8,128)S(1)} %get-tuple-element.5, f32[1,128,2,64]{1,3,0,2:T(8,128)S(1)} %get-tuple-element.14, f32[1,128,2,64]{1,3,0,2:T(8,128)S(1)} %get-tuple-element.13), kind=kOutput, calls=%fused_computation.30 | convolution fusion | flops 12893323264 | bytes 50462720 | tf_op jit(solution)/shard_map/mxkb,xbyq->ymqk/dot_general | solution.py:45
  292.2 19.9 %reshape_reshape.7 = f32[2,1,64,4,8192]{4,3,2,0,1:T(4,128)} reshape(f32[2,256,64,128]{3,2,1,0:T(8,128)} %fusion.25) | data formatting | bytes 33554432 | tf_op jit(solution)/shard_map/reshape;reshape | solution.py:67
  312.2 16.6 %fusion.16 = bf16[2,1,64,4,8192]{4,2,3,1,0:T(8,128)(2,1)} fusion(f32[2,1,64,4,8192]{4,3,2,0,1:T(4,128)} %reshape_reshape.7, f32[64]{0:T(128)S(1)} %convert_multiply_fusion), kind=kLoop, calls=%fused_computation.23 | loop fusion | flops 8388608 | bytes 25166080 | tf_op jit(solution)/shard_map/convert_element_type | solution.py:67
  328.8 24.4 %copy.57 = bf16[2,1,64,4,8192]{2,3,0,1,4:T(4,128)(2,1)} copy(bf16[2,1,64,4,8192]{4,2,3,1,0:T(8,128)(2,1)} %fusion.16) | data formatting | bytes 16777216 | tf_op jit(solution)/shard_map/convert_element_type | solution.py:67
  353.2 26.5 %reshape.228 = bf16[64,2,32768]{2,1,0:T(2,128)(2,1)} reshape(bf16[8192,1,2,4,64]{4,3,2,1,0:T(4,128)(2,1)} %bitcast.68) | data formatting | bytes 16777216
  379.7 108.5 %all_to_all.15 = bf16[64,2,32768]{2,1,0:T(2,128)(2,1)} all-to-all(bf16[64,2,32768]{2,1,0:T(2,128)(2,1)} %reshape.228), channel_id=1, replica_groups=mesh['inp'=8,'tm'=8,'bl'=2] {'inp','tm'}, dimensions={0} | all-to-all | bytes 16777216 | tf_op jit(solution)/shard_map/all_to_all | solution.py:68
  488.2 26.0 %reshape.229 = bf16[8192,1,2,4,64]{4,3,2,1,0:T(4,128)(2,1)} reshape(bf16[64,2,32768]{2,1,0:T(2,128)(2,1)} %all_to_all.15) | data formatting | bytes 16777216
  514.2 23.4 %copy.77 = bf16[2,1,64,4,64,128]{5,2,3,4,0,1:T(8,128)(2,1)} copy(bf16[2,1,64,4,64,128]{2,3,0,5,4,1:T(4,128)(2,1)} %bitcast.69) | data formatting | bytes 16777216 | tf_op jit(solution)/shard_map/all_to_all | solution.py:68
  537.6 27.8 %reshape.219 = bf16[2,8,8,64,4,2,64]{6,5,3,4,2,1,0:T(2,128)(2,1)} reshape(bf16[2,64,1,64,4,128]{5,3,4,1,0,2:T(8,128)(2,1)} %bitcast.71) | data formatting | bytes 16777216 | tf_op jit(solution)/shard_map/reshape | solution.py:75
  565.4 15.2 %copy.60 = bf16[2,8,8,64,4,2,64]{6,3,2,4,1,0,5:T(8,128)(2,1)} copy(bf16[2,8,8,64,4,2,64]{6,5,3,4,2,1,0:T(2,128)(2,1)} %reshape.219) | data formatting | bytes 16777216 | tf_op jit(solution)/shard_map/reshape | solution.py:75
  580.6 54.9 %all-gather.2.cloned.1.call-done = bf16[2,8,8,128,4,2,64]{6,3,2,4,1,0,5:T(8,128)(2,1)} async-done(((bf16[2,8,8,64,4,2,64]{6,3,2,4,1,0,5:T(8,128)(2,1)}), bf16[2,8,8,128,4,2,64]{6,3,2,4,1,0,5:T(8,128)(2,1)}) %all-gather.2.cloned.1.call-update) | async-done | bytes 16777232 | tf_op jit(solution)/shard_map/all_gather | solution.py:80
  635.4 57.3 %fusion.20 = f32[2,2,2,8,64,8,128]{6,4,3,1,5,2,0:T(8,128)} fusion(bf16[2,8,8,64,4,2,64,1,1]{6,5,3,4,2,1,0,8,7:T(2,128)(2,1)} %bitcast.70, bf16[2,8,8,128,4,2,64]{6,3,2,4,1,0,5:T(8,128)(2,1)} %all-gather.2.cloned.1.call-done), kind=kOutput, calls=%fused_computation.29 | convolution fusion | flops 17179869184 | bytes 41943040 | tf_op jit(solution)/shard_map/xatisgk,yctjsgk->gxyaicj/dot_general | solution.py:77
  692.8 10.4 %slice_add_fusion = (f32[2,1,1,8,64,8,128]{6,4,3,1,5,2,0:T(8,128)}, f32[2,1,1,8,64,8,128]{6,4,3,1,5,2,0:T(8,128)S(1)}) fusion(f32[2,2,2,8,64,8,128]{6,4,3,1,5,2,0:T(8,128)} %fusion.20), kind=kLoop, calls=%fused_computation.33 | loop fusion | flops 2097152 | bytes 25165824 | tf_op jit(solution)/shard_map/add | solution.py:83
  703.1 5.5 copy.62
  708.6 1.0 copy.64
  709.6 3.3 copy.63
  712.9 1.0 copy.65
  713.9 4.4 maximum_multiply_fusion
  (12 shorter events, 0.3 us)
Async XLA Ops:
  6.5 628.9 %all-gather.2.cloned.1.call-start = ((), (), s32[]{:S(2)}) async-start(), calls=%async_computation.1 | async-start | bytes 50331648 | tf_op jit(solution)/shard_map/all_gather | solution.py:80
  14.9 139.2 %collective-permute-start = (bf16[64,3,16384]{2,0,1:T(8,128)(2,1)}, bf16[64,3,16384]{2,0,1:T(8,128)(2,1)}, u32[]{:S(2)}, u32[]{:S(2)}) collective-permute-start(bf16[64,3,16384]{2,0,1:T(8,128)(2,1)} %bitcast.67), channel_id=1, source_target_pairs={{2,0},{4,2},{6,4},{8,6},{10,8},{12,10},{14,12},{3,1},{5,3},{7,5},{... | collective-permute-start | bytes 18874376 | tf_op jit(solution)/shard_map/ppermute | solution.py:14
  27.5 18.5 %copy-start.2 = (s32[64]{0:T(128)S(1)}, s32[64]{0:T(128)}, u32[]{:S(2)}) copy-start(s32[64]{0:T(128)} %param.5) | copy-start | bytes 772
  27.5 18.5 %copy-start.1 = (f32[4,16384]{1,0:T(4,128)S(1)}, f32[4,16384]{1,0:T(4,128)}, u32[]{:S(2)}) copy-start(f32[4,16384]{1,0:T(4,128)} %param.4) | copy-start | bytes 786436
  45.1 120.2 %copy-start = (f32[64,4,16384]{2,1,0:T(4,128)S(1)}, f32[64,4,16384]{2,1,0:T(4,128)}, u32[]{:S(2)}) copy-start(f32[64,4,16384]{2,1,0:T(4,128)} %reshape.218) | copy-start | bytes 50331652
Sparse Core Ops, SparseCore 0:
  580.7 54.6 all-gather.1
where the time goes:
time: 737 us; the launch traced here: 725 us
  local copies, waits for them, and re-layouts  227 us (31%)
  waiting for transfers between devices  163 us (22%)
  matrix products  113 us (15%)
  blocking collectives  108 us (15%)
  other arithmetic  99 us (13%)
  between operations  13.7 us (2%)
    all_to_all x1, blocking collectives, shards(): lax.all_to_all(spectra[:, None], ('inp', 'tm'), split_axis=4, concat_axis...  108 us
    ppermute x1, waiting for transfers between devices, passed_along(): lax.ppermute(value, axis, [(source, source + steps) for source in range(i...  108 us
    dot_general x1, matrix products, shards(): jnp.einsum('xatisgk,yctjsgk->gxyaicj', rows, lax.all_gather(rows, 'bl', a...  57.3 us
    all_gather x1, waiting for transfers between devices, shards(): lax.all_gather(rows, 'bl', axis=3, tiled=True)  54.9 us
    unnamed x8, local copies, waits for them, and re-layouts  52.6 us
    reshape x2, local copies, waits for them, and re-layouts, shards(): turned.reshape(2, groups_inp, groups_tm, inputs, spectra_dev, out_groups,...  43 us
    add x1, other arithmetic, shards(): filtered + taps[offset][None, None, :] * extended[:, offset:offset + spec...  32.6 us
    dot_general x1, matrix products, transform(): jnp.einsum('ykn,mnb->mykb', table_one, blocks, precision=highest)  32.5 us
  transfers between devices with their start and end apart: 2, of which 2 were waited for; matrix products, arithmetic and copies ran while one was open for 4% of the time, Pallas kernels for 0%

commit v1 on v0

v1 whole, which is shorter than its diff:
```python
import math

import jax
import jax.numpy as jnp
from jax import lax
from jax.sharding import PartitionSpec as P

CH_AVG = 64
FIRST = 128


def passed_along(value, axis, steps):
    count = lax.axis_size(axis)
    initial, last = (max(0, -steps), min(count, count - steps))
    return lax.ppermute(value, axis, [(source, source + steps) for source in range(initial, last)])


def cos_sin(height, breadth, period):
    grid = lax.broadcasted_iota(jnp.int32, (height, breadth), 0) * lax.broadcasted_iota(
        jnp.int32, (height, breadth), 1
    )
    angle = (grid % period).astype(jnp.float32) * (2.0 * math.pi / period)
    return (jnp.cos(angle), jnp.sin(angle))


def transform(blocks, length, precision):
    first_len = FIRST
    second_len = length // first_len
    highs = length // 2 // first_len
    cos_one, sin_one = cos_sin(first_len, first_len, first_len)
    table_one = jnp.stack([cos_one, -sin_one])
    section_one = jnp.einsum("xca,mab->xmcb", table_one, blocks, precision=precision)
    cos_twist, sin_twist = cos_sin(first_len, second_len, length)
    real_one = section_one[0]
    imag_one = section_one[1]
    twisted = jnp.stack(
        [real_one * cos_twist + imag_one * sin_twist, imag_one * cos_twist - real_one * sin_twist]
    )
    cos_two, sin_two = cos_sin(highs, second_len, second_len)
    table_two = jnp.stack(
        [jnp.stack([cos_two, sin_two], axis=1), jnp.stack([-sin_two, cos_two], axis=1)]
    )
    return jnp.einsum("yqxb,xmcb->yqmc", table_two, twisted, precision=precision)


def shards(voltages, taps, flags):
    inputs = voltages.shape[0]
    tap_count = taps.shape[0]
    length = taps.shape[1]
    spectra_dev = voltages.shape[1] // length
    reach = tap_count - 1
    samples = voltages.astype(jnp.float32).reshape(inputs, spectra_dev, length)
    leading = voltages[:, : reach * length].reshape(inputs, reach, length).astype(jnp.bfloat16)
    following = passed_along(leading, "tm", -1)
    extended = jnp.concatenate([samples, following.astype(jnp.float32)], axis=1)
    filtered = jnp.zeros((inputs, spectra_dev, length), jnp.float32)
    for offset in range(tap_count):
        filtered = (
            filtered + taps[offset][None, None, :] * extended[:, offset : offset + spectra_dev]
        )
    blocks = filtered.reshape(inputs * spectra_dev, FIRST, length // FIRST)
    both_parts = transform(blocks, length, lax.Precision.HIGHEST)
    scale = jnp.repeat(flags.astype(jnp.float32) / (8.0 * math.sqrt(length)), spectra_dev)
    spectra = (both_parts * scale[None, None, :, None]).astype(jnp.bfloat16)
    turned = lax.all_to_all(spectra, ("inp", "tm"), split_axis=1, concat_axis=1, tiled=True)
    groups_inp = lax.axis_size("inp")
    groups_tm = lax.axis_size("tm")
    out_groups = FIRST // CH_AVG
    rows = turned.reshape(2, groups_inp, groups_tm, inputs, spectra_dev, out_groups, CH_AVG)
    own = jnp.transpose(rows, (5, 1, 3, 0, 2, 4, 6)).reshape(out_groups, groups_inp, inputs, -1)
    half = own.shape[-1] // 2
    swapped = jnp.concatenate([own[..., half:], -own[..., :half]], axis=-1)
    lhs = jnp.stack([own, swapped], axis=1).reshape(out_groups, 2, groups_inp * inputs, -1)
    columns = lax.all_gather(own, "bl", axis=2, tiled=True).reshape(out_groups, -1, 2 * half)
    count = float(groups_tm * spectra_dev * CH_AVG)
    products = jnp.einsum("gxpk,gqk->xgpq", lhs, columns, preferred_element_type=jnp.float32)
    visibilities = products * (1.0 / count)
    return visibilities.reshape(2, out_groups, groups_inp, inputs, columns.shape[1])


def solution(mesh):
    in_specs = (P(("inp", "bl"), "tm"), P(), P(("inp", "bl")))
    out_specs = P(None, ("inp", "tm"), None, "bl", None)
    return jax.shard_map(shards, mesh=mesh, in_specs=in_specs, out_specs=out_specs, check_vma=False)
```

time: 737 us -> 575 us (0.78)
  the two profiles are of different devices: /device:TPU:1 before, /device:TPU:2 now
where the time goes in v1:
time: 575 us; the launch traced here: 565 us
  local copies, waits for them, and re-layouts  167 us (29%)
  blocking collectives  110 us (19%)
  waiting for transfers between devices  105 us (18%)
  matrix products  82.6 us (14%)
  other arithmetic  81.2 us (14%)
  between operations  13.7 us (2%)
    all_to_all x1, blocking collectives, shards(): lax.all_to_all(spectra, ('inp', 'tm'), split_axis=1, concat_axis=1, tiled...  110 us
    ppermute x1, waiting for transfers between devices, passed_along(): lax.ppermute(value, axis, [(source, source + steps) for source in range(i...  105 us
    reshape x2, local copies, waits for them, and re-layouts, shards(): turned.reshape(2, groups_inp, groups_tm, inputs, spectra_dev, out_groups,...  41.4 us
    dot_general x1, matrix products, transform(): jnp.einsum('xca,mab->xmcb', table_one, blocks, precision=precision)  32.8 us
    add x1, other arithmetic, shards(): filtered + taps[offset][None, None, :] * extended[:, offset:offset + spec...  32.6 us
    another operation x1, local copies, waits for them, and re-layouts, shards(): jnp.stack([own, swapped], axis=1)  26.8 us
    reshape x1, local copies, waits for them, and re-layouts, shards(): jnp.transpose(rows, (5, 1, 3, 0, 2, 4, 6))  25.6 us
    dot_general x1, matrix products, transform(): jnp.einsum('yqxb,xmcb->yqmc', table_two, twisted, precision=precision)  25 us
  transfers between devices with their start and end apart: 2, of which 1 were waited for; matrix products, arithmetic and copies ran while one was open for 12% of the time, Pallas kernels for 0%

profile of v1, /device:TPU:2, one launch (start us, length us, event | category | flops | bytes accessed | tf_op | source)
XLA Modules:
  0.0 564.7 jit_solution(10519536967132959035)
XLA Ops:
  6.5 0.0 all-gather.2.cloned.1.call-start
  6.5 5.2 slice_convert_fusion
  11.8 3.1 copy.30
  14.9 4.9 collective-permute-start
  19.8 11.3 %convert_element_type.73 = f32[64,65536]{1,0:T(8,128)} convert(s32[64,65536]{1,0:T(8,128)} %param.3) | non-fusion elementwise | flops 4194304 | bytes 33554432 | tf_op jit(solution)/shard_map/convert_element_type | solution.py:52
  31.1 17.6 %reshape.177 = f32[64,4,16384]{2,1,0:T(4,128)} reshape(f32[64,65536]{1,0:T(8,128)} %convert_element_type.73) | data formatting | bytes 33554432 | tf_op jit(solution)/shard_map/reshape | solution.py:52
  48.7 0.0 copy-done.2
  48.7 0.1 broadcast_in_dim.2
  48.8 0.1 mul.242
  48.9 0.1 fusion.50
  49.0 0.1 fusion.48
  49.2 0.3 sine_negate_fusion
  49.5 0.3 fusion.42
  49.8 0.2 fusion.55
  50.0 104.9 %collective-permute-done = bf16[64,3,16384]{2,0,1:T(8,128)(2,1)} collective-permute-done((bf16[64,3,16384]{2,0,1:T(8,128)(2,1)}, bf16[64,3,16384]{2,0,1:T(8,128)(2,1)}, u32[]{:S(2)}, u32[]{:S(2)}) %collective-permute-start) | collective-permute-done | bytes 6291488 | tf_op jit(solution)/shard_map/ppermute | solution.py:15
  154.8 11.2 %copy.12 = f32[64,3,16384]{2,1,0:T(4,128)} copy(bf16[64,3,16384]{2,0,1:T(8,128)(2,1)} %collective-permute-done) | data formatting | bytes 18874368 | tf_op jit(solution)/shard_map/convert_element_type | solution.py:55
  166.1 32.6 %fusion.6 = f32[64,4,16384]{2,1,0:T(4,128)} fusion(f32[64,4,16384]{2,1,0:T(4,128)S(1)} %copy-done, f32[64,3,16384]{2,1,0:T(4,128)} %copy.12, f32[16384]{0:T(1024)S(1)} %bitcast.63, f32[16384]{0:T(1024)S(1)} %bitcast.64, f32[16384]{0:T(1024)S(1)} %bitcast.62, f32[16384]{0:T(1024)S(1)} %bitcast.61), kind=kLoop, calls=%fused_computation.11 | loop fusion | flops 41943040 | bytes 46399488 | tf_op jit(solution)/shard_map/add | solution.py:59
  198.6 20.5 %reshape.178 = f32[256,128,128]{2,1,0:T(8,128)} reshape(f32[64,4,16384]{2,1,0:T(4,128)} %fusion.6) | data formatting | bytes 33554432 | tf_op jit(solution)/shard_map/reshape | solution.py:61
  219.2 32.8 %fusion.18 = f32[2,256,128,128]{2,3,0,1:T(8,128)} fusion(f32[256,128,128]{2,1,0:T(8,128)} %reshape.178, f32[1,128,128]{2,1,0:T(8,128)S(1)} %get-tuple-element.15, f32[1,128,128]{2,1,0:T(8,128)S(1)} %get-tuple-element.16), kind=kOutput, calls=%fused_computation.28 | convolution fusion | flops 12884934656 | bytes 50462720 | tf_op jit(solution)/shard_map/xca,mab->xmcb/dot_general | solution.py:32
  251.9 17.8 %multiply_add_fusion = (f32[1,256,128,128]{2,3,0,1:T(8,128)S(1)}, f32[1,256,128,128]{2,3,0,1:T(8,128)}) fusion(f32[2,256,128,128]{2,3,0,1:T(8,128)} %fusion.18, f32[128,128]{0,1:T(8,128)S(1)} %get-tuple-element.17, f32[128,128]{0,1:T(8,128)S(1)} %get-tuple-element.18), kind=kLoop, calls=%fused_computation.27 | loop fusion | flops 25165824 | bytes 67239936 | tf_op jit(solution)/shard_map/add | solution.py:37
  269.7 25.0 %fusion.17 = bf16[2,64,256,128]{3,1,2,0:T(8,128)(2,1)} fusion(f32[256]{0:T(256)S(1)} %mul.242, f32[1,256,128,128]{2,3,0,1:T(8,128)} %get-tuple-element.6, f32[1,256,128,128]{2,3,0,1:T(8,128)S(1)} %get-tuple-element.5, f32[1,64,2,128]{3,1,2,0:T(8,128)S(1)} %get-tuple-element.14, f32[1,64,2,128]{3,1,2,0:T(8,128)S(1)} %get-tuple-element.13), kind=kOutput, calls=%fused_computation.24 | convolution fusion | flops 12901711872 | bytes 42075136 | tf_op jit(solution)/shard_map/yqxb,xmcb->yqmc/dot_general | solution.py:43
  294.7 12.0 %copy.15 = bf16[2,64,256,128]{3,2,0,1:T(8,128)(2,1)} copy(bf16[2,64,256,128]{3,1,2,0:T(8,128)(2,1)} %fusion.17) | data formatting | bytes 16777216 | tf_op jit(solution)/shard_map/convert_element_type | solution.py:64
  306.7 110.2 %all_to_all.5 = bf16[2,64,256,128]{3,2,0,1:T(8,128)(2,1)} all-to-all(bf16[2,64,256,128]{3,2,0,1:T(8,128)(2,1)} %copy.15), channel_id=1, replica_groups=mesh['inp'=8,'tm'=8,'bl'=2] {'inp','tm'}, dimensions={1} | all-to-all | bytes 16777216 | tf_op jit(solution)/shard_map/all_to_all | solution.py:65
  416.9 27.8 %reshape.179 = bf16[2,8,8,64,4,2,64]{6,5,4,3,0,2,1:T(2,128)(2,1)} reshape(bf16[2,64,256,128]{3,2,0,1:T(8,128)(2,1)} %all_to_all.5) | data formatting | bytes 16777216 | tf_op jit(solution)/shard_map/reshape | solution.py:69
  444.7 13.6 %copy.29 = bf16[2,8,8,64,4,2,64]{6,4,2,0,3,1,5:T(4,128)(2,1)} copy(bf16[2,8,8,64,4,2,64]{6,5,4,3,0,2,1:T(2,128)(2,1)} %reshape.179) | data formatting | bytes 16777216 | tf_op jit(solution)/shard_map/reshape | solution.py:69
  458.3 25.6 %reshape.180 = bf16[2,8,64,4096]{3,2,1,0:T(8,128)(2,1)} reshape(bf16[2,8,64,2,8,4,64]{6,5,4,3,2,1,0:T(4,128)(2,1)} %bitcast.56) | data formatting | bytes 16777216 | tf_op jit(solution)/shard_map/reshape | solution.py:70
  483.9 0.0 all-gather.2.cloned.1.call-update
  484.0 26.8 %stack.44 = bf16[2,1,512,4096]{3,2,1,0:T(8,128)(2,1)} reshape(bf16[2,8,64,2,8,4,64]{6,5,4,3,2,1,0:T(4,128)(2,1)} %bitcast.57) | data formatting | bytes 16777216 | tf_op jit(solution)/shard_map/stack | solution.py:73
  510.8 5.7 %fusion.54 = (bf16[2,8,64,2048]{3,2,1,0:T(8,128)(2,1)}, bf16[2,8,64,2048]{3,2,1,0:T(8,128)(2,1)}) fusion(bf16[2,8,64,4096]{3,2,1,0:T(8,128)(2,1)} %reshape.180), kind=kLoop, calls=%fused_computation.80 | loop fusion | flops 2097152 | bytes 16777216 | tf_op jit(solution)/shard_map/slice | solution.py:72
  516.5 7.8 %pad_maximum_fusion.1 = bf16[2,8,64,4096]{3,2,1,0:T(8,128)(2,1)} fusion(bf16[2,8,64,2048]{3,2,1,0:T(8,128)(2,1)} %get-tuple-element.8, bf16[2,8,64,2048]{3,2,1,0:T(8,128)(2,1)} %get-tuple-element.7), kind=kLoop, calls=%fused_computation.30 | loop fusion | flops 16777216 | bytes 16777216 | tf_op jit(solution)/shard_map/concatenate | solution.py:72
  524.3 24.9 %broadcast_multiply_fusion = f32[2,1024,2,512]{1,3,2,0:T(8,128)} fusion(bf16[2,1024,4096,1]{2,1,3,0:T(8,128)(2,1)} %bitcast.65, bf16[2,1,512,4096]{3,2,1,0:T(8,128)(2,1)} %bitcast.59, bf16[2,1,512,4096]{3,2,1,0:T(8,128)(2,1)} %stack.44), kind=kOutput, calls=%fused_computation.33 | convolution fusion | flops 17215520768 | bytes 41943040 | tf_op jit(solution)/shard_map/gxpk,gqk->xgpq/dot_general | solution.py:76
  549.2 8.4 %copy.17 = f32[2,2,8,64,1024]{4,3,2,1,0:T(8,128)} copy(f32[2,2,8,64,1024]{4,3,2,0,1:T(8,128)} %bitcast.60) | data formatting | bytes 16777216 | tf_op jit(solution)/shard_map/reshape | solution.py:78
  (8 shorter events, 0.0 us)
Async XLA Ops:
  6.5 517.8 %all-gather.2.cloned.1.call-start = ((), (), s32[]{:S(2)}) async-start(), calls=%async_computation.1 | async-start | bytes 25165824 | tf_op jit(solution)/shard_map/all_gather | solution.py:74
  14.9 140.0 %collective-permute-start = (bf16[64,3,16384]{2,0,1:T(8,128)(2,1)}, bf16[64,3,16384]{2,0,1:T(8,128)(2,1)}, u32[]{:S(2)}, u32[]{:S(2)}) collective-permute-start(bf16[64,3,16384]{2,0,1:T(8,128)(2,1)} %bitcast.55), channel_id=1, source_target_pairs={{2,0},{4,2},{6,4},{8,6},{10,8},{12,10},{14,12},{3,1},{5,3},{7,5},{... | collective-permute-start | bytes 18874376 | tf_op jit(solution)/shard_map/ppermute | solution.py:15
  31.1 17.6 %copy-start.2 = (s32[64]{0:T(128)S(1)}, s32[64]{0:T(128)}, u32[]{:S(2)}) copy-start(s32[64]{0:T(128)} %param.5) | copy-start | bytes 772
  31.1 18.7 %copy-start.1 = (f32[4,16384]{1,0:T(4,128)S(1)}, f32[4,16384]{1,0:T(4,128)}, u32[]{:S(2)}) copy-start(f32[4,16384]{1,0:T(4,128)} %param.4) | copy-start | bytes 786436
  48.9 117.2 %copy-start = (f32[64,4,16384]{2,1,0:T(4,128)S(1)}, f32[64,4,16384]{2,1,0:T(4,128)}, u32[]{:S(2)}) copy-start(f32[64,4,16384]{2,1,0:T(4,128)} %reshape.177) | copy-start | bytes 50331652
Sparse Core Ops, SparseCore 0:
  484.1 29.5 all-gather.1

commit v2 on v1

--- a/solution.py
+++ b/solution.py
@@ -53,29 +53,40 @@
     leading = voltages[:, : reach * length].reshape(inputs, reach, length).astype(jnp.bfloat16)
     following = passed_along(leading, "tm", -1)
     extended = jnp.concatenate([samples, following.astype(jnp.float32)], axis=1)
-    filtered = jnp.zeros((inputs, spectra_dev, length), jnp.float32)
-    for offset in range(tap_count):
-        filtered = (
-            filtered + taps[offset][None, None, :] * extended[:, offset : offset + spectra_dev]
-        )
-    blocks = filtered.reshape(inputs * spectra_dev, FIRST, length // FIRST)
-    both_parts = transform(blocks, length, lax.Precision.HIGHEST)
+
+    def filtered(source, first, count):
+        total = jnp.zeros((inputs, count, length), jnp.float32)
+        for offset in range(tap_count):
+            start = first + offset
+            total = total + taps[offset][None, None, :] * source[:, start : start + count]
+        return total.reshape(inputs * count, FIRST, length // FIRST)
+
+    local = spectra_dev - reach
+    parts = [transform(filtered(samples, 0, local), length, lax.Precision.HIGH)]
+    parts.append(transform(filtered(extended, local, reach), length, lax.Precision.HIGH))
+    highs = parts[0].shape[1]
+    both_parts = jnp.concatenate(
+        [parts[0].reshape(2, highs, inputs, local, FIRST), parts[1].reshape(2, highs, inputs, reach, FIRST)],
+        axis=3,
+    ).reshape(2, highs, inputs * spectra_dev, FIRST)
     scale = jnp.repeat(flags.astype(jnp.float32) / (8.0 * math.sqrt(length)), spectra_dev)
-    spectra = (both_parts * scale[None, None, :, None]).astype(jnp.bfloat16)
-    turned = lax.all_to_all(spectra, ("inp", "tm"), split_axis=1, concat_axis=1, tiled=True)
+    spectra = both_parts * scale[None, None, :, None]
+    out_groups = FIRST // CH_AVG
+    spectra = spectra.reshape(2, highs, inputs, spectra_dev, out_groups, CH_AVG)
+    spectra = jnp.transpose(spectra, (1, 4, 2, 0, 3, 5)).reshape(highs, out_groups, inputs, -1)
+    spectra = spectra.astype(jnp.bfloat16)
+    turned = lax.all_to_all(spectra, ("inp", "tm"), split_axis=0, concat_axis=0, tiled=True)
     groups_inp = lax.axis_size("inp")
     groups_tm = lax.axis_size("tm")
-    out_groups = FIRST // CH_AVG
-    rows = turned.reshape(2, groups_inp, groups_tm, inputs, spectra_dev, out_groups, CH_AVG)
-    own = jnp.transpose(rows, (5, 1, 3, 0, 2, 4, 6)).reshape(out_groups, groups_inp, inputs, -1)
+    own = turned.reshape(groups_inp, groups_tm, out_groups, inputs, -1)
     half = own.shape[-1] // 2
     swapped = jnp.concatenate([own[..., half:], -own[..., :half]], axis=-1)
-    lhs = jnp.stack([own, swapped], axis=1).reshape(out_groups, 2, groups_inp * inputs, -1)
-    columns = lax.all_gather(own, "bl", axis=2, tiled=True).reshape(out_groups, -1, 2 * half)
+    lhs = jnp.stack([own, swapped])
+    columns = lax.all_gather(own, "bl", axis=3, tiled=True)
     count = float(groups_tm * spectra_dev * CH_AVG)
-    products = jnp.einsum("gxpk,gqk->xgpq", lhs, columns, preferred_element_type=jnp.float32)
+    products = jnp.einsum("xptgik,qtgjk->xgpiqj", lhs, columns, preferred_element_type=jnp.float32)
     visibilities = products * (1.0 / count)
-    return visibilities.reshape(2, out_groups, groups_inp, inputs, columns.shape[1])
+    return visibilities.reshape(2, out_groups, groups_inp, inputs, -1)
 
 
 def solution(mesh):

time: 575 us -> 587 us (1.021)
  the two profiles are of different devices: /device:TPU:2 before, /device:TPU:1 now
where the time goes in v2:
time: 587 us; the launch traced here: 576 us
  local copies, waits for them, and re-layouts  171 us (29%)
  other arithmetic  146 us (25%)
  blocking collectives  108 us (18%)
  waiting for transfers between devices  69.4 us (12%)
  matrix products  67 us (11%)
  between operations  13.7 us (2%)
    all_to_all x1, blocking collectives, shards(): lax.all_to_all(spectra, ('inp', 'tm'), split_axis=0, concat_axis=0, tiled...  108 us
    concatenate x4, local copies, waits for them, and re-layouts, shards(): jnp.concatenate([parts[0].reshape(2, highs, inputs, local, FIRST), parts[...  71 us
    add x2, other arithmetic, filtered(): total = total + taps[offset][None, None, :] * source[:, start:start + count]  56.5 us
    ppermute x1, waiting for transfers between devices, passed_along(): lax.ppermute(value, axis, [(source, source + steps) for source in range(i...  50.8 us
    convert_element_type x1, local copies, waits for them, and re-layouts, shards(): spectra = spectra.astype(jnp.bfloat16)  26.4 us
    dot_general x1, matrix products, shards(): jnp.einsum('xptgik,qtgjk->xgpiqj', lhs, columns, preferred_element_type=j...  25 us
    convert_element_type x1, other arithmetic, shards(): spectra = spectra.astype(jnp.bfloat16)  23.2 us
    add x2, other arithmetic, transform(): real_one * cos_twist + imag_one * sin_twist  21.6 us
  transfers between devices with their start and end apart: 2, of which 2 were waited for; matrix products, arithmetic and copies ran while one was open for 18% of the time, Pallas kernels for 0%

profile of v2, /device:TPU:1, one launch (start us, length us, event | category | flops | bytes accessed | tf_op | source)
XLA Modules:
  0.0 575.9 jit_solution(10290565394965478333)
XLA Ops:
  6.5 5.2 slice_convert_fusion
  11.8 3.0 copy.57
  14.8 1.3 collective-permute-start
  16.3 11.3 %convert_element_type.90 = f32[64,65536]{1,0:T(8,128)} convert(s32[64,65536]{1,0:T(8,128)} %param.3) | non-fusion elementwise | flops 4194304 | bytes 33554432 | tf_op jit(solution)/shard_map/convert_element_type | solution.py:52
  27.5 17.6 %reshape.194 = f32[64,4,16384]{2,1,0:T(4,128)} reshape(f32[64,65536]{1,0:T(8,128)} %convert_element_type.90) | data formatting | bytes 33554432 | tf_op jit(solution)/shard_map/reshape | solution.py:52
  45.4 0.3 fusion.46
  45.7 0.3 sine_negate_fusion
  46.0 26.2 %fusion.25 = f32[64,1,16384]{2,1,0:T(1,128)S(1)} fusion(f32[64,4,16384]{2,1,0:T(4,128)} %reshape.194, f32[16384]{0:T(1024)S(1)} %bitcast.103, f32[16384]{0:T(1024)S(1)} %bitcast.105, f32[16384]{0:T(1024)S(1)} %bitcast.101, f32[16384]{0:T(1024)S(1)} %bitcast.99), kind=kLoop, calls=%fused_computation.40 | loop fusion | flops 7340032 | bytes 21233664 | tf_op jit(solution)/shard_map/add | solution.py:61
  72.3 3.5 convolution_bitcast_fusion
  75.7 1.9 multiply_add_fusion.1
  77.6 4.4 fusion.30
  82.0 9.3 %concatenate.14 = f32[2,64,64,1,2,64]{5,4,1,2,0,3:T(2,128)} reshape(f32[2,64,64,128]{3,1,2,0:T(8,128)} %fusion.30) | data formatting | bytes 8388608 | tf_op jit(solution)/shard_map/concatenate | solution.py:68
  91.3 11.8 %copy.33 = f32[2,64,64,1,2,64]{5,3,0,2,4,1:T(1,128)} copy(f32[2,64,64,1,2,64]{5,4,1,2,0,3:T(2,128)} %concatenate.14) | data formatting | bytes 8388608 | tf_op jit(solution)/shard_map/concatenate | solution.py:68
  103.2 50.8 %collective-permute-done = bf16[64,3,16384]{2,0,1:T(8,128)(2,1)} collective-permute-done((bf16[64,3,16384]{2,0,1:T(8,128)(2,1)}, bf16[64,3,16384]{2,0,1:T(8,128)(2,1)}, u32[]{:S(2)}, u32[]{:S(2)}) %collective-permute-start) | collective-permute-done | bytes 6291488 | tf_op jit(solution)/shard_map/ppermute | solution.py:15
  154.0 11.2 %copy_convert_fusion = f32[64,3,16384]{2,1,0:T(4,128)} fusion(bf16[64,3,16384]{2,0,1:T(8,128)(2,1)} %collective-permute-done), kind=kLoop, calls=%fused_computation.35 | loop fusion | flops 3145728 | bytes 18874368 | tf_op jit(solution)/shard_map/convert_element_type | solution.py:55
  165.2 30.2 %fusion.9 = f32[64,3,16384]{2,1,0:T(4,128)} fusion(f32[64,4,16384]{2,1,0:T(4,128)S(1)} %bitcast.93, f32[64,3,16384]{2,1,0:T(4,128)} %copy_convert_fusion, f32[16384]{0:T(1024)S(1)} %bitcast.104, f32[16384]{0:T(1024)S(1)} %bitcast.106, f32[16384]{0:T(1024)S(1)} %bitcast.102, f32[16384]{0:T(1024)S(1)} %bitcast.100), kind=kLoop, calls=%fused_computation.13 | loop fusion | flops 28311552 | bytes 58982400 | tf_op jit(solution)/shard_map/add | solution.py:61
  195.5 21.1 %reshape.196 = f32[192,128,128]{2,1,0:T(8,128)} reshape(f32[64,3,16384]{2,1,0:T(4,128)} %fusion.9) | data formatting | bytes 25165824 | tf_op jit(solution)/shard_map/reshape | solution.py:62
  216.6 17.7 %fusion.17 = f32[2,192,128,128]{2,3,0,1:T(8,128)} fusion(f32[192,128,128]{2,1,0:T(8,128)} %reshape.196, f32[1,128,128]{2,1,0:T(8,128)S(1)} %get-tuple-element.17, f32[1,128,128]{2,1,0:T(8,128)S(1)} %get-tuple-element.18), kind=kOutput, calls=%fused_computation.27 | convolution fusion | flops 4831870976 | bytes 37879808 | tf_op jit(solution)/shard_map/xca,mab->xmcb/dot_general | solution.py:32
  234.2 19.7 %multiply_add_fusion = (f32[1,192,128,128]{2,3,0,1:T(8,128)}, f32[1,192,128,128]{2,3,0,1:T(8,128)}) fusion(f32[2,192,128,128]{2,3,0,1:T(8,128)} %fusion.17, f32[128,128]{0,1:T(8,128)S(1)} %get-tuple-element.19, f32[128,128]{0,1:T(8,128)S(1)} %get-tuple-element.20), kind=kLoop, calls=%fused_computation.26 | loop fusion | flops 18874368 | bytes 50462720 | tf_op jit(solution)/shard_map/add | solution.py:37
  253.9 16.5 %fusion.24 = f32[2,64,192,128]{3,1,2,0:T(8,128)} fusion(f32[1,192,128,128]{2,3,0,1:T(8,128)} %get-tuple-element.6, f32[1,192,128,128]{2,3,0,1:T(8,128)} %get-tuple-element.5, f32[1,64,2,128]{3,1,2,0:T(8,128)S(1)} %get-tuple-element.16, f32[1,64,2,128]{3,1,2,0:T(8,128)S(1)} %get-tuple-element.15), kind=kOutput, calls=%fused_computation.37 | convolution fusion | flops 4838162432 | bytes 37879808 | tf_op jit(solution)/shard_map/yqxb,xmcb->yqmc/dot_general | solution.py:43
  270.4 25.1 %concatenate.16 = f32[2,64,64,3,2,64]{5,4,1,3,2,0:T(2,128)} reshape(f32[2,64,192,128]{3,1,2,0:T(8,128)} %fusion.24) | data formatting | bytes 25165824 | tf_op jit(solution)/shard_map/concatenate | solution.py:68
  295.4 24.8 %copy.34 = f32[2,64,64,3,2,64]{5,3,0,2,4,1:T(4,128)} copy(f32[2,64,64,3,2,64]{5,4,1,3,2,0:T(2,128)} %concatenate.16) | data formatting | bytes 25165824 | tf_op jit(solution)/shard_map/concatenate | solution.py:68
  320.3 23.2 %fusion.4 = bf16[64,2,64,2,4,64]{5,4,3,2,1,0:T(4,128)(2,1)} fusion(f32[2,64,64,3,2,64]{5,3,0,2,4,1:T(4,128)} %copy.34, f32[2,64,64,1,2,64]{5,3,0,2,4,1:T(1,128)} %copy.33, f32[64]{0:T(128)S(1)} %convert_multiply_fusion), kind=kLoop, calls=%fused_computation.8 | loop fusion | flops 12582912 | bytes 25166080 | tf_op jit(solution)/shard_map/convert_element_type | solution.py:77
  343.5 26.4 %convert_element_type.98 = bf16[64,2,64,512]{3,2,1,0:T(8,128)(2,1)} reshape(bf16[64,2,64,2,4,64]{5,4,3,2,1,0:T(4,128)(2,1)} %fusion.4) | data formatting | bytes 16777216 | tf_op jit(solution)/shard_map/convert_element_type | solution.py:77
  369.9 108.0 %all_to_all.5 = bf16[64,2,64,512]{3,2,1,0:T(8,128)(2,1)} all-to-all(bf16[64,2,64,512]{3,2,1,0:T(8,128)(2,1)} %convert_element_type.98), channel_id=1, replica_groups=mesh['inp'=8,'tm'=8,'bl'=2] {'inp','tm'}, dimensions={0} | all-to-all | bytes 16777216 | tf_op jit(solution)/shard_map/all_to_all | solution.py:78
  477.9 7.9 %copy.35 = bf16[64,2,64,512]{3,2,0,1:T(8,128)(2,1)} copy(bf16[64,2,64,512]{3,2,1,0:T(8,128)(2,1)} %all_to_all.5) | data formatting | bytes 16777216 | tf_op jit(solution)/shard_map/all_to_all | solution.py:78
  485.8 5.7 fusion.60
  491.5 10.1 %maximum_bitcast_fusion.6 = bf16[1,8,8,2,64,512]{5,4,2,1,0,3:T(8,128)(2,1)} fusion(bf16[8,8,2,64,256]{4,3,1,0,2:T(8,128)(2,1)} %get-tuple-element.10, bf16[8,8,2,64,256]{4,3,1,0,2:T(8,128)(2,1)} %get-tuple-element.9), kind=kLoop, calls=%fused_computation.32 | loop fusion | flops 16777216 | bytes 16777216 | tf_op jit(solution)/shard_map/stack | solution.py:84
  501.6 18.6 %all-gather.2.cloned.1.call-done = bf16[8,8,2,128,512]{4,3,1,0,2:T(8,128)(2,1)} async-done(((bf16[8,8,2,64,512]{4,3,1,0,2:T(8,128)(2,1)}), bf16[8,8,2,128,512]{4,3,1,0,2:T(8,128)(2,1)}) %all-gather.2.cloned.1.call-update) | async-done | bytes 16777232 | tf_op jit(solution)/shard_map/all_gather | solution.py:85
  520.2 25.0 %fusion.23 = f32[2,2,8,64,8,128]{5,3,2,0,4,1:T(8,128)} fusion(bf16[1,8,8,2,64,512]{5,4,2,1,0,3:T(8,128)(2,1)} %maximum_bitcast_fusion.6, bf16[1,8,8,2,64,512]{5,4,2,1,0,3:T(8,128)(2,1)} %bitcast.96, bf16[8,8,2,128,512]{4,3,1,0,2:T(8,128)(2,1)} %all-gather.2.cloned.1.call-done), kind=kOutput, calls=%fused_computation.34 | convolution fusion | flops 17215520768 | bytes 41943040 | tf_op jit(solution)/shard_map/xptgik,qtgjk->xgpiqj/dot_general | solution.py:87
  545.3 14.3 %copy.37 = f32[2,2,8,64,8,128]{5,4,3,2,1,0:T(8,128)} copy(f32[2,2,8,64,8,128]{5,3,2,0,4,1:T(8,128)} %fusion.23) | data formatting | bytes 16777216 | tf_op jit(solution)/shard_map/mul | solution.py:88
  559.6 9.2 %reshape.198 = f32[2,2,8,64,1024]{4,3,2,1,0:T(8,128)} reshape(f32[2,2,8,64,8,128]{5,4,3,2,1,0:T(8,128)} %copy.37) | data formatting | bytes 16777216 | tf_op jit(solution)/shard_map/reshape | solution.py:89
  (20 shorter events, 0.5 us)
Async XLA Ops:
  6.5 9.5 %copy-start = (f32[4,16384]{1,0:T(4,128)S(1)}, f32[4,16384]{1,0:T(4,128)}, u32[]{:S(2)}) copy-start(f32[4,16384]{1,0:T(4,128)} %param.4) | copy-start | bytes 786436
  6.5 513.7 %all-gather.2.cloned.1.call-start = ((), (), s32[]{:S(2)}) async-start(), calls=%async_computation.1 | async-start | bytes 25165824 | tf_op jit(solution)/shard_map/all_gather | solution.py:85
  14.8 139.2 %collective-permute-start = (bf16[64,3,16384]{2,0,1:T(8,128)(2,1)}, bf16[64,3,16384]{2,0,1:T(8,128)(2,1)}, u32[]{:S(2)}, u32[]{:S(2)}) collective-permute-start(bf16[64,3,16384]{2,0,1:T(8,128)(2,1)} %bitcast.91), channel_id=1, source_target_pairs={{2,0},{4,2},{6,4},{8,6},{10,8},{12,10},{14,12},{3,1},{5,3},{7,5},{... | collective-permute-start | bytes 18874376 | tf_op jit(solution)/shard_map/ppermute | solution.py:15
  82.0 21.1 %copy-start.1 = (s32[64]{0:T(128)S(1)}, s32[64]{0:T(128)}, u32[]{:S(2)}) copy-start(s32[64]{0:T(128)} %param.5) | copy-start | bytes 772
  91.3 73.9 %slice-start = ((s8[16777216]{0:T(1024)(128)(4,1)}), s8[4194304]{0:T(1024)(128)(4,1)S(1)}, s32[]{:S(2)}) async-start(s8[16777216]{0:T(1024)(128)(4,1)} %bitcast.92), calls=%async_computation.2 | async-start | bytes 8388608
  91.3 73.9 %slice-start.1 = ((s8[16777216]{0:T(1024)(128)(4,1)}), s8[4194304]{0:T(1024)(128)(4,1)S(1)}, s32[]{:S(2)}) async-start(s8[16777216]{0:T(1024)(128)(4,1)} %bitcast.92), calls=%async_computation.3 | async-start | bytes 8388608
  103.1 62.1 %slice-start.2 = ((s8[16777216]{0:T(1024)(128)(4,1)}), s8[4194304]{0:T(1024)(128)(4,1)S(1)}, s32[]{:S(2)}) async-start(s8[16777216]{0:T(1024)(128)(4,1)} %bitcast.92), calls=%async_computation.4 | async-start | bytes 8388608
  103.1 62.1 %slice-start.3 = ((s8[16777216]{0:T(1024)(128)(4,1)}), s8[4194304]{0:T(1024)(128)(4,1)S(1)}, s32[]{:S(2)}) async-start(s8[16777216]{0:T(1024)(128)(4,1)} %bitcast.92), calls=%async_computation.5 | async-start | bytes 8388608
Sparse Core Ops, SparseCore 0:
  486.0 34.2 all-gather.1

commit v3 on v1

--- a/solution.py
+++ b/solution.py
@@ -47,35 +47,49 @@
     inputs = voltages.shape[0]
     tap_count = taps.shape[0]
     length = taps.shape[1]
+    second_len = length // FIRST
     spectra_dev = voltages.shape[1] // length
     reach = tap_count - 1
-    samples = voltages.astype(jnp.float32).reshape(inputs, spectra_dev, length)
-    leading = voltages[:, : reach * length].reshape(inputs, reach, length).astype(jnp.bfloat16)
+    local = spectra_dev - reach
+    precision = lax.Precision.HIGH
+    blocked = voltages.reshape(inputs, spectra_dev, FIRST, second_len)
+    leading = blocked[:, :reach].astype(jnp.bfloat16)
     following = passed_along(leading, "tm", -1)
-    extended = jnp.concatenate([samples, following.astype(jnp.float32)], axis=1)
-    filtered = jnp.zeros((inputs, spectra_dev, length), jnp.float32)
-    for offset in range(tap_count):
-        filtered = (
-            filtered + taps[offset][None, None, :] * extended[:, offset : offset + spectra_dev]
-        )
-    blocks = filtered.reshape(inputs * spectra_dev, FIRST, length // FIRST)
-    both_parts = transform(blocks, length, lax.Precision.HIGHEST)
-    scale = jnp.repeat(flags.astype(jnp.float32) / (8.0 * math.sqrt(length)), spectra_dev)
+    samples = blocked.astype(jnp.float32)
+    tap_blocks = taps.reshape(tap_count, FIRST, second_len)
+
+    def filtered(pieces, count):
+        rows = []
+        for spectrum in range(count):
+            total = jnp.zeros((inputs, FIRST, second_len), jnp.float32)
+            for offset in range(tap_count):
+                total = total + tap_blocks[offset][None] * pieces[spectrum + offset]
+            rows.append(total)
+        return jnp.concatenate(rows, axis=0)
+
+    own_pieces = [samples[:, j] for j in range(spectra_dev)]
+    next_pieces = [following[:, j].astype(jnp.float32) for j in range(reach)]
+    first_part = transform(filtered(own_pieces, local), length, precision)
+    second_part = transform(filtered(own_pieces[local:] + next_pieces, reach), length, precision)
+    both_parts = jnp.concatenate([first_part, second_part], axis=2)
+    scale = jnp.tile(flags.astype(jnp.float32) / (8.0 * math.sqrt(length)), spectra_dev)
     spectra = (both_parts * scale[None, None, :, None]).astype(jnp.bfloat16)
     turned = lax.all_to_all(spectra, ("inp", "tm"), split_axis=1, concat_axis=1, tiled=True)
     groups_inp = lax.axis_size("inp")
     groups_tm = lax.axis_size("tm")
     out_groups = FIRST // CH_AVG
-    rows = turned.reshape(2, groups_inp, groups_tm, inputs, spectra_dev, out_groups, CH_AVG)
-    own = jnp.transpose(rows, (5, 1, 3, 0, 2, 4, 6)).reshape(out_groups, groups_inp, inputs, -1)
+    rows = turned.reshape(2, groups_inp, groups_tm, spectra_dev, inputs, FIRST)
+    own = jnp.transpose(rows, (1, 4, 0, 2, 3, 5)).reshape(groups_inp, inputs, -1)
     half = own.shape[-1] // 2
     swapped = jnp.concatenate([own[..., half:], -own[..., :half]], axis=-1)
-    lhs = jnp.stack([own, swapped], axis=1).reshape(out_groups, 2, groups_inp * inputs, -1)
-    columns = lax.all_gather(own, "bl", axis=2, tiled=True).reshape(out_groups, -1, 2 * half)
+    lane_group = (lax.broadcasted_iota(jnp.int32, (out_groups, own.shape[-1]), 1) % FIRST) // CH_AVG
+    mask = (lane_group == lax.broadcasted_iota(jnp.int32, (out_groups, own.shape[-1]), 0))
+    mask = mask.astype(own.dtype)
+    lhs = jnp.stack([own, swapped])[:, None] * mask[None, :, None, None, :]
+    columns = lax.all_gather(own, "bl", axis=1, tiled=True).reshape(-1, own.shape[-1])
     count = float(groups_tm * spectra_dev * CH_AVG)
-    products = jnp.einsum("gxpk,gqk->xgpq", lhs, columns, preferred_element_type=jnp.float32)
-    visibilities = products * (1.0 / count)
-    return visibilities.reshape(2, out_groups, groups_inp, inputs, columns.shape[1])
+    products = jnp.einsum("xgpik,qk->xgpiq", lhs, columns, preferred_element_type=jnp.float32)
+    return products * (1.0 / count)
 
 
 def solution(mesh):

time: 575 us -> 509 us (0.89)
  the two profiles are of different devices: /device:TPU:2 before, /device:TPU:1 now
where the time goes in v3:
time: 509 us; the launch traced here: 503 us
  local copies, waits for them, and re-layouts  113 us (22%)
  blocking collectives  108 us (21%)
  other arithmetic  92.8 us (18%)
  matrix products  89.4 us (18%)
  waiting for transfers between devices  84.5 us (17%)
  between operations  13.8 us (3%)
    all_to_all x1, blocking collectives, shards(): lax.all_to_all(spectra, ('inp', 'tm'), split_axis=1, concat_axis=1, tiled...  108 us
    ppermute x1, waiting for transfers between devices, passed_along(): lax.ppermute(value, axis, [(source, source + steps) for source in range(i...  84.4 us
    unnamed x19, local copies, waits for them, and re-layouts  49.5 us
    dot_general x1, matrix products, shards(): jnp.einsum('xgpik,qk->xgpiq', lhs, columns, preferred_element_type=jnp.fl...  42.5 us
    dot_general x2, matrix products, transform(): jnp.einsum('xca,mab->xmcb', table_one, blocks, precision=precision)  26 us
    another operation x2, other arithmetic, shards(): lhs = jnp.stack([own, swapped])[:, None] * mask[None, :, None, None, :]  23.2 us
    unnamed x1, other arithmetic  21.8 us
    dot_general x2, matrix products, transform(): jnp.einsum('yqxb,xmcb->yqmc', table_two, twisted, precision=precision)  21 us
  transfers between devices with their start and end apart: 2, of which 1 were waited for; matrix products, arithmetic and copies ran while one was open for 20% of the time, Pallas kernels for 0%

profile of v3, /device:TPU:1, one launch (start us, length us, event | category | flops | bytes accessed | tf_op | source)
XLA Modules:
  0.0 503.2 jit_solution(362682598263856912)
XLA Ops:
  6.5 21.8 %convert_bitcast_fusion.1 = (bf16[8,8,512,128]{3,1,2,0:T(8,128)(2,1)}, f32[8,8,512,128]{3,1,2,0:T(8,128)}) fusion(s32[64,65536]{1,0:T(8,128)} %param.3), kind=kLoop, calls=%fused_computation.27 | loop fusion | flops 8388608 | bytes 41943040
  28.3 9.0 %copy.51 = bf16[8,8,512,128]{3,2,1,0:T(8,128)(2,1)} copy(bf16[8,8,512,128]{3,1,2,0:T(8,128)(2,1)} %get-tuple-element.11) | data formatting | bytes 16777216
  37.3 8.1 %slice.95 = bf16[64,3,128,128]{3,2,1,0:T(8,128)(2,1)} slice(bf16[64,4,128,128]{3,2,1,0:T(8,128)(2,1)} %bitcast.155), slice={[0:64], [0:3], [0:128], [0:128]} | slice | bytes 12582912 | tf_op jit(solution)/shard_map/slice | solution.py:56
  45.4 8.6 %copy.49 = bf16[64,3,128,128]{2,3,0,1:T(8,128)(2,1)} copy(bf16[64,3,128,128]{3,2,1,0:T(8,128)(2,1)} %slice.95) | data formatting | bytes 12582912
  54.0 1.6 collective-permute-start
  55.6 9.4 %copy.50 = f32[8,8,512,128]{3,2,1,0:T(8,128)S(1)} copy(f32[8,8,512,128]{3,1,2,0:T(8,128)} %get-tuple-element.12) | data formatting | bytes 33554432
  65.0 6.0 %fusion.77 = (f32[64,1,128,128]{3,2,1,0:T(8,128)}, f32[64,1,128,128]{3,2,1,0:T(8,128)}, f32[64,1,128,128]{3,2,1,0:T(8,128)}, f32[64,1,128,128]{3,2,1,0:T(8,128)}) fusion(f32[64,4,128,128]{3,2,1,0:T(8,128)S(1)} %bitcast.153), kind=kLoop, calls=%fused_computation.128 | loop fusion | bytes 33554432 | tf_op jit(solution)/shard_map/slice | solution.py:70
  71.0 5.6 %copy.46 = f32[64,1,128,128]{2,3,0,1:T(8,128)} copy(f32[64,1,128,128]{3,2,1,0:T(8,128)} %get-tuple-element.9) | data formatting | bytes 8388608
  76.6 5.7 %copy.47 = f32[64,1,128,128]{2,3,0,1:T(8,128)} copy(f32[64,1,128,128]{3,2,1,0:T(8,128)} %get-tuple-element.8) | data formatting | bytes 8388608
  82.3 5.6 %copy.48 = f32[64,1,128,128]{2,3,0,1:T(8,128)} copy(f32[64,1,128,128]{3,2,1,0:T(8,128)} %get-tuple-element.10) | data formatting | bytes 8388608
  87.9 5.6 %copy.45 = f32[64,1,128,128]{2,3,0,1:T(8,128)} copy(f32[64,1,128,128]{3,2,1,0:T(8,128)} %get-tuple-element.7) | data formatting | bytes 8388608
  94.6 0.3 sine_negate_fusion
  94.9 0.3 fusion.63
  95.2 8.0 %fusion.37 = f32[2,64,128,128]{2,3,0,1:T(8,128)S(1)} fusion(f32[64,1,128,128]{2,3,0,1:T(8,128)} %copy.48, f32[64,1,128,128]{2,3,0,1:T(8,128)} %copy.47, f32[64,1,128,128]{2,3,0,1:T(8,128)} %copy.46, f32[64,1,128,128]{2,3,0,1:T(8,128)} %copy.45, f32[128,128]{0,1:T(8,128)S(1)} %copy.28, f32[128,128]{0,1:T(8,128)S(1)} %copy.26, f32[128,128]{0,1:T(8,128)S(1)} %copy.24, ...), kind=kOutput, calls=%fused_computation.63 | convolution fusion | flops 1617985536 | bytes 25559040 | tf_op jit(solution)/shard_map/xca,mab->xmcb/dot_general | solution.py:32
  103.1 1.2 multiply_add_fusion.1
  104.4 4.4 fusion.40
  108.7 84.4 %collective-permute-done = bf16[64,3,128,128]{2,3,0,1:T(8,128)(2,1)} collective-permute-done((bf16[64,3,128,128]{2,3,0,1:T(8,128)(2,1)}, bf16[64,3,128,128]{2,3,0,1:T(8,128)(2,1)}, u32[]{:S(2)}, u32[]{:S(2)}) %collective-permute-start) | collective-permute-done | bytes 6291488 | tf_op jit(solution)/shard_map/ppermute | solution.py:15
  193.2 8.2 %fusion.21 = (f32[64,128,128]{1,2,0:T(8,128)}, f32[64,128,128]{1,2,0:T(8,128)}, f32[64,128,128]{1,2,0:T(8,128)}) fusion(f32[64,1,128,128]{2,3,0,1:T(8,128)S(1)} %copy-done.2, f32[64,1,128,128]{2,3,0,1:T(8,128)S(1)} %copy-done.1, f32[64,1,128,128]{2,3,0,1:T(8,128)S(1)} %copy-done, f32[128,128]{0,1:T(8,128)S(1)} %copy.28, f32[128,128]{0,1:T(8,128)S(1)} %copy.26, ...), kind=kLoop, calls=%fused_computation.37 | loop fusion | flops 25165824 | bytes 31719424 | tf_op jit(solution)/shard_map/add | solution.py:66
  201.4 18.0 %fusion.13 = f32[2,192,128,128]{2,3,0,1:T(8,128)} fusion(f32[64,128,128]{1,2,0:T(8,128)} %get-tuple-element.15, f32[64,128,128]{1,2,0:T(8,128)} %get-tuple-element.14, f32[64,128,128]{1,2,0:T(8,128)} %get-tuple-element.13, f32[1,128,128]{2,1,0:T(8,128)S(1)} %get-tuple-element.26, f32[1,128,128]{2,1,0:T(8,128)S(1)} %get-tuple-element.27), kind=kOutput, calls=%fused_computation.20 | convolution fusion | flops 4838162432 | bytes 37879808 | tf_op jit(solution)/shard_map/xca,mab->xmcb/dot_general | solution.py:32
  219.4 19.8 %multiply_add_fusion = (f32[1,192,128,128]{2,3,0,1:T(8,128)}, f32[1,192,128,128]{2,3,0,1:T(8,128)}) fusion(f32[2,192,128,128]{2,3,0,1:T(8,128)} %fusion.13, f32[128,128]{0,1:T(8,128)S(1)} %get-tuple-element.28, f32[128,128]{0,1:T(8,128)S(1)} %get-tuple-element.29), kind=kLoop, calls=%fused_computation.19 | loop fusion | flops 18874368 | bytes 50462720 | tf_op jit(solution)/shard_map/add | solution.py:37
  239.2 16.6 %fusion.17 = f32[2,64,192,128]{3,1,2,0:T(8,128)} fusion(f32[1,192,128,128]{2,3,0,1:T(8,128)} %get-tuple-element.6, f32[1,192,128,128]{2,3,0,1:T(8,128)} %get-tuple-element.5, f32[1,64,2,128]{3,1,2,0:T(8,128)S(1)} %get-tuple-element.25, f32[1,64,2,128]{3,1,2,0:T(8,128)S(1)} %get-tuple-element.24), kind=kOutput, calls=%fused_computation.33 | convolution fusion | flops 4838162432 | bytes 37879808 | tf_op jit(solution)/shard_map/yqxb,xmcb->yqmc/dot_general | solution.py:43
  255.8 9.0 %fusion.5 = bf16[2,64,256,128]{3,1,2,0:T(8,128)(2,1)} fusion(f32[2,64,192,128]{3,1,2,0:T(8,128)} %fusion.17, f32[2,64,64,128]{3,1,2,0:T(8,128)S(1)} %copy-done.3, f32[256]{0:T(256)S(1)} %mul.388), kind=kLoop, calls=%fused_computation.7 | loop fusion | flops 12582912 | bytes 25166848 | tf_op jit(solution)/shard_map/convert_element_type | solution.py:76
  264.8 12.0 %copy.33 = bf16[2,64,256,128]{3,2,0,1:T(8,128)(2,1)} copy(bf16[2,64,256,128]{3,1,2,0:T(8,128)(2,1)} %fusion.5) | data formatting | bytes 16777216 | tf_op jit(solution)/shard_map/convert_element_type | solution.py:76
  276.9 108.1 %all_to_all.5 = bf16[2,64,256,128]{3,2,0,1:T(8,128)(2,1)S(1)} all-to-all(bf16[2,64,256,128]{3,2,0,1:T(8,128)(2,1)} %copy.33), channel_id=1, replica_groups=mesh['inp'=8,'tm'=8,'bl'=2] {'inp','tm'}, dimensions={1} | all-to-all | bytes 16777216 | tf_op jit(solution)/shard_map/all_to_all | solution.py:77
  385.0 7.3 %copy.53 = bf16[2,8,8,4,64,128]{5,3,2,0,4,1:T(4,128)(2,1)} copy(bf16[2,8,8,4,64,128]{5,4,3,0,2,1:T(8,128)(2,1)S(1)} %bitcast.154) | data formatting | bytes 16777216 | tf_op jit(solution)/shard_map/reshape | solution.py:81
  392.3 14.4 %reshape.241 = bf16[8,64,8192]{2,1,0:T(8,128)(2,1)} reshape(bf16[8,64,2,8,4,128]{5,4,3,2,1,0:T(4,128)(2,1)} %bitcast.151) | data formatting | bytes 16777216 | tf_op jit(solution)/shard_map/reshape | solution.py:82
  406.8 0.2 compare_convert_fusion
  407.0 14.9 %stack_reshape.3 = bf16[1,8,64,8192]{3,2,1,0:T(8,128)(2,1)} reshape(bf16[8,64,2,8,4,128]{5,4,3,2,1,0:T(4,128)(2,1)} %bitcast.152) | data formatting | bytes 16777216 | tf_op jit(solution)/shard_map/stack;reshape | solution.py:88
  421.9 8.6 %fusion.78 = (bf16[8,64,4096]{2,1,0:T(8,128)(2,1)}, bf16[8,64,4096]{2,1,0:T(8,128)(2,1)}) fusion(bf16[8,64,8192]{2,1,0:T(8,128)(2,1)} %reshape.241), kind=kLoop, calls=%fused_computation.129 | loop fusion | flops 2097152 | bytes 16777216 | tf_op jit(solution)/shard_map/slice | solution.py:84
  430.5 9.4 %maximum_bitcast_fusion.8 = bf16[1,8,64,8192]{3,2,1,0:T(8,128)(2,1)} fusion(bf16[8,64,4096]{2,1,0:T(8,128)(2,1)} %get-tuple-element.19, bf16[8,64,4096]{2,1,0:T(8,128)(2,1)} %get-tuple-element.18), kind=kLoop, calls=%fused_computation.25 | loop fusion | flops 16777216 | bytes 16777216 | tf_op jit(solution)/shard_map/stack | solution.py:88
  439.9 13.8 %pad_maximum_fusion = bf16[2,8,64,8192]{3,2,1,0:T(8,128)(2,1)} fusion(bf16[1,8,64,8192]{3,2,1,0:T(8,128)(2,1)} %maximum_bitcast_fusion.8, bf16[1,8,64,8192]{3,2,1,0:T(8,128)(2,1)} %stack_reshape.3), kind=kLoop, calls=%fused_computation.8 | loop fusion | flops 8388608 | bytes 33554432 | tf_op jit(solution)/shard_map/stack | solution.py:88
  453.7 42.5 %broadcast_multiply_fusion = f32[2,2,8,64,1024]{4,3,2,1,0:T(8,128)} fusion(bf16[1024,8192,1,1,1]{1,0,4,3,2:T(8,128)(2,1)} %bitcast.160, bf16[2,8192]{1,0:T(2,128)(2,1)S(1)} %compare_convert_fusion, bf16[2,8,64,8192]{3,2,1,0:T(8,128)(2,1)} %pad_maximum_fusion), kind=kOutput, calls=%fused_computation.60 | convolution fusion | flops 34378612736 | bytes 41975808 | tf_op jit(solution)/shard_map/xgpik,qk->xgpiq/dot_general | solution.py:91
  (28 shorter events, 1.0 us)
Async XLA Ops:
  6.5 447.1 %all-gather.2.cloned.1.call-start = ((), (), s32[]{:S(2)}) async-start(), calls=%async_computation.1 | async-start | bytes 25165824 | tf_op jit(solution)/shard_map/all_gather | solution.py:89
  54.0 139.2 %collective-permute-start = (bf16[64,3,128,128]{2,3,0,1:T(8,128)(2,1)}, bf16[64,3,128,128]{2,3,0,1:T(8,128)(2,1)}, u32[]{:S(2)}, u32[]{:S(2)}) collective-permute-start(bf16[64,3,128,128]{2,3,0,1:T(8,128)(2,1)} %copy.49), channel_id=1, source_target_pairs={{2,0},{4,2},{6,4},{8,6},{10,8},{12,10},{14,12},{3,1},{5,3},{7,5},{... | collective-permute-start | bytes 18874376 | tf_op jit(solution)/shard_map/ppermute | solution.py:15
  87.9 5.6 %copy-start.4 = (f32[4,16384]{1,0:T(4,128)S(1)}, f32[4,16384]{1,0:T(4,128)}, u32[]{:S(2)}) copy-start(f32[4,16384]{1,0:T(4,128)} %param.4) | copy-start | bytes 786436
  87.9 6.2 %copy-start.5 = (s32[64]{0:T(128)S(1)}, s32[64]{0:T(128)}, u32[]{:S(2)}) copy-start(s32[64]{0:T(128)} %param.5) | copy-start | bytes 772
  104.3 88.9 %copy-start = (f32[64,1,128,128]{2,3,0,1:T(8,128)S(1)}, f32[64,1,128,128]{2,3,0,1:T(8,128)}, u32[]{:S(2)}) copy-start(f32[64,1,128,128]{2,3,0,1:T(8,128)} %copy.46) | copy-start | bytes 12582916
  104.3 88.9 %copy-start.1 = (f32[64,1,128,128]{2,3,0,1:T(8,128)S(1)}, f32[64,1,128,128]{2,3,0,1:T(8,128)}, u32[]{:S(2)}) copy-start(f32[64,1,128,128]{2,3,0,1:T(8,128)} %copy.47) | copy-start | bytes 12582916
  104.3 88.9 %copy-start.2 = (f32[64,1,128,128]{2,3,0,1:T(8,128)S(1)}, f32[64,1,128,128]{2,3,0,1:T(8,128)}, u32[]{:S(2)}) copy-start(f32[64,1,128,128]{2,3,0,1:T(8,128)} %copy.48) | copy-start | bytes 12582916
  239.2 16.6 %copy-start.3 = (f32[2,64,64,128]{3,1,2,0:T(8,128)S(1)}, f32[2,64,64,128]{3,1,2,0:T(8,128)}, u32[]{:S(2)}) copy-start(f32[2,64,64,128]{3,1,2,0:T(8,128)} %fusion.40) | copy-start | bytes 12582916
Sparse Core Ops, SparseCore 0:
  406.9 33.5 all-gather.1

commit v4 on v3

--- a/solution.py
+++ b/solution.py
@@ -3,6 +3,8 @@
 import jax
 import jax.numpy as jnp
 from jax import lax
+from jax.experimental import pallas as pl
+from jax.experimental.pallas import tpu as pltpu
 from jax.sharding import PartitionSpec as P
 
 CH_AVG = 64
@@ -43,6 +45,83 @@
     return jnp.einsum("yqxb,xmcb->yqmc", table_two, twisted, precision=precision)
 
 
+def correlate(own, gathered, prior, scale):
+    _, groups_inp, groups_tm, count_s, inputs, lanes = own.shape
+    rows = groups_inp * inputs
+    cols = gathered.shape[1] * gathered.shape[4]
+    depth = groups_tm * lanes
+    out_groups = lanes // CH_AVG
+
+    def kernel(*refs):
+        own_ref, gat_ref = refs[0], refs[1]
+        out_ref = refs[-1]
+        group = pl.program_id(0)
+        spectrum = pl.program_id(1)
+
+        @pl.when(spectrum == 0)
+        def _():
+            if prior is None:
+                out_ref[...] = jnp.zeros(out_ref.shape, out_ref.dtype)
+            else:
+                out_ref[...] = refs[2][...]
+
+        def chunks(ref, part):
+            pieces = [ref[part, :, t, 0].reshape(-1, lanes) for t in range(groups_tm)]
+            return jnp.concatenate(pieces, axis=1)
+
+        x0, x1 = chunks(own_ref, 0), chunks(own_ref, 1)
+        c0, c1 = chunks(gat_ref, 0), chunks(gat_ref, 1)
+        low = (lax.broadcasted_iota(jnp.int32, (1, depth), 1) % lanes) < CH_AVG
+
+        def near(value, upper):
+            return pltpu.roll(value, depth - CH_AVG if upper else CH_AVG, 1)
+
+        def accumulate(upper):
+            if upper:
+                left_re = jnp.where(low, near(x0, True), x1)
+                left_im = jnp.where(low, near(x1, True), -x0)
+                right = jnp.where(low, near(c0, True), c1)
+            else:
+                left_re = jnp.where(low, x0, near(x1, False))
+                left_im = jnp.where(low, x1, -near(x0, False))
+                right = jnp.where(low, c0, near(c1, False))
+            dims = (((1,), (1,)), ((), ()))
+            real = lax.dot_general(left_re, right, dims, preferred_element_type=jnp.float32)
+            imag = lax.dot_general(left_im, right, dims, preferred_element_type=jnp.float32)
+            out_ref[0, 0] += real * scale
+            out_ref[1, 0] += imag * scale
+
+        for g in range(out_groups):
+            pl.when(group == g)(lambda g=g: accumulate(g == 1))
+
+    block_own = (2, groups_inp, groups_tm, 1, inputs, lanes)
+    block_gat = (2, groups_inp, groups_tm, 1, gathered.shape[4], lanes)
+    out_block = (2, 1, rows, cols)
+    in_specs = [
+        pl.BlockSpec(block_own, lambda g, s: (0, 0, 0, s, 0, 0)),
+        pl.BlockSpec(block_gat, lambda g, s: (0, 0, 0, s, 0, 0)),
+    ]
+    operands = [own, gathered]
+    aliases = {}
+    if prior is not None:
+        in_specs.append(pl.BlockSpec(out_block, lambda g, s: (0, g, 0, 0)))
+        operands.append(prior)
+        aliases = {2: 0}
+    flops = 2 * 2 * rows * cols * depth * count_s * out_groups
+    return pl.pallas_call(
+        kernel,
+        grid=(out_groups, count_s),
+        in_specs=in_specs,
+        out_specs=pl.BlockSpec(out_block, lambda g, s: (0, g, 0, 0)),
+        out_shape=jax.ShapeDtypeStruct((2, out_groups, rows, cols), jnp.float32),
+        input_output_aliases=aliases,
+        compiler_params=pltpu.CompilerParams(vmem_limit_bytes=60 * 1024 * 1024),
+        cost_estimate=pl.CostEstimate(
+            flops=flops, transcendentals=0, bytes_accessed=2 * (own.size + gathered.size) * out_groups + 8 * rows * cols * out_groups
+        ),
+    )(*operands)
+
+
 def shards(voltages, taps, flags):
     inputs = voltages.shape[0]
     tap_count = taps.shape[0]
@@ -67,29 +146,26 @@
             rows.append(total)
         return jnp.concatenate(rows, axis=0)
 
+    scale = flags.astype(jnp.float32) / (8.0 * math.sqrt(length))
+    groups_inp = lax.axis_size("inp")
+    groups_tm = lax.axis_size("tm")
+    count = float(groups_tm * spectra_dev * CH_AVG)
+
+    def corner_turn(parts, count_s):
+        spectra = (parts * jnp.tile(scale, count_s)[None, None, :, None]).astype(jnp.bfloat16)
+        turned = lax.all_to_all(spectra, ("inp", "tm"), split_axis=1, concat_axis=1, tiled=True)
+        own = turned.reshape(2, groups_inp, groups_tm, count_s, inputs, FIRST)
+        return own, lax.all_gather(own, "bl", axis=4, tiled=True)
+
     own_pieces = [samples[:, j] for j in range(spectra_dev)]
     next_pieces = [following[:, j].astype(jnp.float32) for j in range(reach)]
     first_part = transform(filtered(own_pieces, local), length, precision)
+    own, gathered = corner_turn(first_part, local)
+    visibilities = correlate(own, gathered, None, 1.0 / count)
     second_part = transform(filtered(own_pieces[local:] + next_pieces, reach), length, precision)
-    both_parts = jnp.concatenate([first_part, second_part], axis=2)
-    scale = jnp.tile(flags.astype(jnp.float32) / (8.0 * math.sqrt(length)), spectra_dev)
-    spectra = (both_parts * scale[None, None, :, None]).astype(jnp.bfloat16)
-    turned = lax.all_to_all(spectra, ("inp", "tm"), split_axis=1, concat_axis=1, tiled=True)
-    groups_inp = lax.axis_size("inp")
-    groups_tm = lax.axis_size("tm")
-    out_groups = FIRST // CH_AVG
-    rows = turned.reshape(2, groups_inp, groups_tm, spectra_dev, inputs, FIRST)
-    own = jnp.transpose(rows, (1, 4, 0, 2, 3, 5)).reshape(groups_inp, inputs, -1)
-    half = own.shape[-1] // 2
-    swapped = jnp.concatenate([own[..., half:], -own[..., :half]], axis=-1)
-    lane_group = (lax.broadcasted_iota(jnp.int32, (out_groups, own.shape[-1]), 1) % FIRST) // CH_AVG
-    mask = (lane_group == lax.broadcasted_iota(jnp.int32, (out_groups, own.shape[-1]), 0))
-    mask = mask.astype(own.dtype)
-    lhs = jnp.stack([own, swapped])[:, None] * mask[None, :, None, None, :]
-    columns = lax.all_gather(own, "bl", axis=1, tiled=True).reshape(-1, own.shape[-1])
-    count = float(groups_tm * spectra_dev * CH_AVG)
-    products = jnp.einsum("xgpik,qk->xgpiq", lhs, columns, preferred_element_type=jnp.float32)
-    return products * (1.0 / count)
+    own, gathered = corner_turn(second_part, reach)
+    visibilities = correlate(own, gathered, visibilities, 1.0 / count)
+    return visibilities.reshape(2, FIRST // CH_AVG, groups_inp, inputs, -1)
 
 
 def solution(mesh):

time: 509 us -> 448 us (0.88)
  blocking collectives: 108 us -> 0 us
  waiting for transfers between devices: 84.5 us -> 179 us
  matrix products: 89.4 us -> 45.2 us
  other arithmetic: 92.8 us -> 55.1 us
  Pallas kernels: 0 us -> 37.4 us
  local copies, waits for them, and re-layouts: 113 us -> 83.9 us
  starting transfers between devices: 1.57 us -> 29 us
    all_to_all x1 -> x0, blocking collectives: 108 us -> none  [shards(): lax.all_to_all(spectra, ('inp', 'tm'), split_axis=1, concat_axis=1, tiled...]
    all_to_all x0 -> x2, waiting for transfers between devices: none -> 71.5 us  [corner_turn(): lax.all_to_all(spectra, ('inp', 'tm'), split_axis=1, concat_axis=1, tiled...]
    dot_general x1 -> x0, matrix products: 42.5 us -> none  [shards(): jnp.einsum('xgpik,qk->xgpiq', lhs, columns, preferred_element_type=jnp.fl...]
    pallas_call x0 -> x2, Pallas kernels: none -> 37.4 us  [correlate(): pl.pallas_call(kernel, grid=(out_groups, count_s), in_specs=in_specs, out...]
    all_to_all x0 -> x2, starting transfers between devices: none -> 27.4 us  [corner_turn(): lax.all_to_all(spectra, ('inp', 'tm'), split_axis=1, concat_axis=1, tiled...]
    all_gather x1 -> x2, waiting for transfers between devices: 0.01 us -> 24.2 us  [corner_turn(): return (own, lax.all_gather(own, 'bl', axis=4, tiled=True))]
    another operation x2 -> x0, other arithmetic: 23.2 us -> none  [shards(): lhs = jnp.stack([own, swapped])[:, None] * mask[None, :, None, None, :]]
    reshape x2 -> x0, local copies, waits for them, and re-layouts: 21.7 us -> none  [the longest x1 14.4 us: shards(): jnp.transpose(rows, (1, 4, 0, 2, 3, 5)).reshape(groups_inp, inputs, -1)]
  transfers between devices with their start and end apart: 2 -> 5, of which waited for: 1 -> 3; matrix products, arithmetic and copies ran while one was open for 20% -> 31% of each run, Pallas kernels for 0% -> 3%
where the time goes in v4:
time: 448 us; the launch traced here: 444 us
  waiting for transfers between devices  179 us (40%)
  local copies, waits for them, and re-layouts  83.9 us (19%)
  other arithmetic  55.1 us (12%)
  matrix products  45.2 us (10%)
  Pallas kernels  37.4 us (8%)
  starting transfers between devices  29 us (6%)
  between operations  13.8 us (3%)
    ppermute x1, waiting for transfers between devices, passed_along(): lax.ppermute(value, axis, [(source, source + steps) for source in range(i...  83.3 us
    all_to_all x2, waiting for transfers between devices, corner_turn(): lax.all_to_all(spectra, ('inp', 'tm'), split_axis=1, concat_axis=1, tiled...  71.5 us
    unnamed x11, local copies, waits for them, and re-layouts  49.6 us
    pallas_call x2, Pallas kernels, correlate(): pl.pallas_call(kernel, grid=(out_groups, count_s), in_specs=in_specs, out...  37.4 us
    all_to_all x2, starting transfers between devices, corner_turn(): lax.all_to_all(spectra, ('inp', 'tm'), split_axis=1, concat_axis=1, tiled...  27.4 us
    dot_general x2, matrix products, transform(): jnp.einsum('xca,mab->xmcb', table_one, blocks, precision=precision)  25.6 us
    all_gather x2, waiting for transfers between devices, corner_turn(): return (own, lax.all_gather(own, 'bl', axis=4, tiled=True))  24.2 us
    unnamed x1, other arithmetic  21.8 us
  transfers between devices with their start and end apart: 5, of which 3 were waited for; matrix products, arithmetic and copies ran while one was open for 31% of the time, Pallas kernels for 3%

profile of v4, /device:TPU:1, one launch (start us, length us, event | category | flops | bytes accessed | tf_op | source)
XLA Modules:
  0.0 443.5 jit_solution(2730842256548935575)
XLA Ops:
  6.5 21.8 %convert_bitcast_fusion.1 = (bf16[8,8,512,128]{3,1,2,0:T(8,128)(2,1)}, f32[8,8,512,128]{3,1,2,0:T(8,128)}) fusion(s32[64,65536]{1,0:T(8,128)} %param.3), kind=kLoop, calls=%fused_computation.20 | loop fusion | flops 8388608 | bytes 41943040
  28.3 9.0 %copy.56 = bf16[8,8,512,128]{3,2,1,0:T(8,128)(2,1)} copy(bf16[8,8,512,128]{3,1,2,0:T(8,128)(2,1)} %get-tuple-element.11) | data formatting | bytes 16777216
  37.3 8.1 %slice.84 = bf16[64,3,128,128]{3,2,1,0:T(8,128)(2,1)} slice(bf16[64,4,128,128]{3,2,1,0:T(8,128)(2,1)} %bitcast.147), slice={[0:64], [0:3], [0:128], [0:128]} | slice | bytes 12582912 | tf_op jit(solution)/shard_map/slice | solution.py:135
  45.4 8.6 %copy.53 = bf16[64,3,128,128]{2,3,0,1:T(8,128)(2,1)} copy(bf16[64,3,128,128]{3,2,1,0:T(8,128)(2,1)} %slice.84) | data formatting | bytes 12582912
  54.0 1.6 collective-permute-start
  55.6 9.4 %copy.55 = f32[8,8,512,128]{3,2,1,0:T(8,128)S(1)} copy(f32[8,8,512,128]{3,1,2,0:T(8,128)} %get-tuple-element.12) | data formatting | bytes 33554432
  65.0 6.0 %fusion.64 = (f32[64,1,128,128]{3,2,1,0:T(8,128)}, f32[64,1,128,128]{3,2,1,0:T(8,128)}, f32[64,1,128,128]{3,2,1,0:T(8,128)}, f32[64,1,128,128]{3,2,1,0:T(8,128)}) fusion(f32[64,4,128,128]{3,2,1,0:T(8,128)S(1)} %bitcast.146), kind=kLoop, calls=%fused_computation.106 | loop fusion | bytes 33554432 | tf_op jit(solution)/shard_map/slice | solution.py:160
  71.1 5.6 %copy.50 = f32[64,1,128,128]{2,3,0,1:T(8,128)} copy(f32[64,1,128,128]{3,2,1,0:T(8,128)} %get-tuple-element.10) | data formatting | bytes 8388608
  76.7 5.6 %copy.51 = f32[64,1,128,128]{2,3,0,1:T(8,128)} copy(f32[64,1,128,128]{3,2,1,0:T(8,128)} %get-tuple-element.9) | data formatting | bytes 8388608
  82.3 5.7 %copy.52 = f32[64,1,128,128]{2,3,0,1:T(8,128)} copy(f32[64,1,128,128]{3,2,1,0:T(8,128)} %get-tuple-element.8) | data formatting | bytes 8388608
  87.9 5.7 %copy.54 = f32[64,1,128,128]{2,3,0,1:T(8,128)} copy(f32[64,1,128,128]{3,2,1,0:T(8,128)} %get-tuple-element.7) | data formatting | bytes 8388608
  93.6 0.2 fusion.65
  94.5 0.3 sine_negate_fusion
  94.8 0.3 fusion.51
  95.1 7.9 %fusion.29 = f32[2,64,128,128]{2,3,0,1:T(8,128)S(1)} fusion(f32[64,1,128,128]{2,3,0,1:T(8,128)} %copy.54, f32[64,1,128,128]{2,3,0,1:T(8,128)} %copy.52, f32[64,1,128,128]{2,3,0,1:T(8,128)} %copy.51, f32[64,1,128,128]{2,3,0,1:T(8,128)} %copy.50, f32[128,128]{0,1:T(8,128)S(1)} %copy.32, f32[128,128]{0,1:T(8,128)S(1)} %copy.30, f32[128,128]{0,1:T(8,128)S(1)} %copy.28, ...), kind=kOutput, calls=%fused_computation.55 | convolution fusion | flops 1617985536 | bytes 25559040 | tf_op jit(solution)/shard_map/xca,mab->xmcb/dot_general | solution.py:34
  103.0 1.9 multiply_add_fusion.1
  104.9 3.3 fusion.21
  108.2 2.7 copy.39
  110.9 15.8 %all-to-all-start.1 = ((bf16[2,64,64,128]{3,2,0,1:T(8,128)(2,1)}), bf16[2,64,64,128]{3,2,0,1:T(8,128)(2,1)S(1)}, u32[]{:S(2)}, u32[]{:S(2)}) async-start(bf16[2,64,64,128]{3,2,0,1:T(8,128)(2,1)} %copy.39), calls=%async_computation.1 | async-start | bytes 4194304 | tf_op jit(solution)/shard_map/all_to_all | solution.py:156
  126.7 83.3 %collective-permute-done = bf16[64,3,128,128]{2,3,0,1:T(8,128)(2,1)} collective-permute-done((bf16[64,3,128,128]{2,3,0,1:T(8,128)(2,1)}, bf16[64,3,128,128]{2,3,0,1:T(8,128)(2,1)}, u32[]{:S(2)}, u32[]{:S(2)}) %collective-permute-start) | collective-permute-done | bytes 6291488 | tf_op jit(solution)/shard_map/ppermute | solution.py:17
  210.1 10.8 %fusion.16 = (f32[64,128,128]{1,2,0:T(8,128)}, f32[64,128,128]{1,2,0:T(8,128)}, f32[64,128,128]{1,2,0:T(8,128)}) fusion(f32[64,1,128,128]{2,3,0,1:T(8,128)} %copy.52, f32[64,1,128,128]{2,3,0,1:T(8,128)} %copy.51, f32[64,1,128,128]{2,3,0,1:T(8,128)} %copy.50, f32[128,128]{0,1:T(8,128)S(1)} %copy.32, f32[128,128]{0,1:T(8,128)S(1)} %copy.30, ...), kind=kLoop, calls=%fused_computation.29 | loop fusion | flops 25165824 | bytes 31719424 | tf_op jit(solution)/shard_map/add | solution.py:145
  220.9 17.7 %fusion.9 = f32[2,192,128,128]{2,3,0,1:T(8,128)} fusion(f32[64,128,128]{1,2,0:T(8,128)} %get-tuple-element.15, f32[64,128,128]{1,2,0:T(8,128)} %get-tuple-element.14, f32[64,128,128]{1,2,0:T(8,128)} %get-tuple-element.13, f32[1,128,128]{2,1,0:T(8,128)S(1)} %get-tuple-element.24, f32[1,128,128]{2,1,0:T(8,128)S(1)} %get-tuple-element.25), kind=kOutput, calls=%fused_computation.15 | convolution fusion | flops 4838162432 | bytes 37879808 | tf_op jit(solution)/shard_map/xca,mab->xmcb/dot_general | solution.py:34
  238.6 19.7 %multiply_add_fusion = (f32[1,192,128,128]{2,3,0,1:T(8,128)}, f32[1,192,128,128]{2,3,0,1:T(8,128)}) fusion(f32[2,192,128,128]{2,3,0,1:T(8,128)} %fusion.9, f32[128,128]{0,1:T(8,128)S(1)} %get-tuple-element.26, f32[128,128]{0,1:T(8,128)S(1)} %get-tuple-element.27), kind=kLoop, calls=%fused_computation.14 | loop fusion | flops 18874368 | bytes 50462720 | tf_op jit(solution)/shard_map/add | solution.py:39
  258.3 16.4 %fusion.8 = bf16[2,64,192,128]{3,1,2,0:T(8,128)(2,1)} fusion(f32[192]{0:T(256)S(1)} %mul.367, f32[1,192,128,128]{2,3,0,1:T(8,128)} %get-tuple-element.6, f32[1,192,128,128]{2,3,0,1:T(8,128)} %get-tuple-element.5, f32[1,64,2,128]{3,1,2,0:T(8,128)S(1)} %get-tuple-element.23, f32[1,64,2,128]{3,1,2,0:T(8,128)S(1)} %get-tuple-element.22), kind=kOutput, calls=%fused_computation.12 | convolution fusion | flops 4844453888 | bytes 31589120 | tf_op jit(solution)/shard_map/yqxb,xmcb->yqmc/dot_general | solution.py:45
  274.7 9.4 %copy.35 = bf16[2,64,192,128]{3,2,0,1:T(8,128)(2,1)} copy(bf16[2,64,192,128]{3,1,2,0:T(8,128)(2,1)} %fusion.8) | data formatting | bytes 12582912 | tf_op jit(solution)/shard_map/convert_element_type | solution.py:155
  284.1 11.6 %all-to-all-start = ((bf16[2,64,192,128]{3,2,0,1:T(8,128)(2,1)}), bf16[2,64,192,128]{3,2,0,1:T(8,128)(2,1)}, u32[]{:S(2)}, u32[]{:S(2)}) async-start(bf16[2,64,192,128]{3,2,0,1:T(8,128)(2,1)} %copy.35), calls=%async_computation | async-start | bytes 12582912 | tf_op jit(solution)/shard_map/all_to_all | solution.py:156
  295.8 1.6 copy.40
  297.4 71.5 %all-to-all-done = bf16[2,64,192,128]{3,2,0,1:T(8,128)(2,1)} async-done(((bf16[2,64,192,128]{3,2,0,1:T(8,128)(2,1)}), bf16[2,64,192,128]{3,2,0,1:T(8,128)(2,1)}, u32[]{:S(2)}, u32[]{:S(2)}) %all-to-all-start) | async-done | bytes 6291488 | tf_op jit(solution)/shard_map/all_to_all | solution.py:156
  368.9 5.9 %copy.36 = bf16[2,64,192,128]{3,2,1,0:T(8,128)(2,1)} copy(bf16[2,64,192,128]{3,2,0,1:T(8,128)(2,1)} %all-to-all-done) | data formatting | bytes 12582912 | tf_op jit(solution)/shard_map/all_to_all | solution.py:156
  374.9 11.5 %shard_map.37.refs_2_ = f32[2,2,512,1024]{3,2,1,0:T(8,128)} custom-call(bf16[2,8,8,1,64,128]{5,4,3,2,1,0:T(8,128)(2,1)} %bitcast.151, bf16[2,8,8,1,128,128]{5,4,3,2,1,0:T(8,128)(2,1)} %all-gather.5.cloned.1.call-done.refs_1_), custom_call_target="tpu_custom_call" | custom-call | flops 4294967296 | bytes 20971520 | tf_op jit(solution)/shard_map/pallas_call | solution.py:111
  386.4 24.2 %all-gather.3.cloned.1.call-done.refs_1_ = bf16[2,8,8,3,128,128]{5,4,3,2,1,0:T(8,128)(2,1)} async-done(((bf16[2,8,8,3,64,128]{5,4,3,2,1,0:T(8,128)(2,1)}), bf16[2,8,8,3,128,128]{5,4,3,2,1,0:T(8,128)(2,1)}) %all-gather.3.cloned.1.call-update) | async-done | bytes 12582928 | tf_op jit(solution)/shard_map/all_gather | solution.py:158
  410.6 25.9 %shard_map.38 = f32[2,2,512,1024]{3,2,1,0:T(8,128)} custom-call(bf16[2,8,8,3,64,128]{5,4,3,2,1,0:T(8,128)(2,1)} %bitcast.149, bf16[2,8,8,3,128,128]{5,4,3,2,1,0:T(8,128)(2,1)} %all-gather.3.cloned.1.call-done.refs_1_, f32[2,2,512,1024]{3,2,1,0:T(8,128)} %shard_map.37.refs_2_), custom_call_target="tpu_custom_call", output_to_operand_aliasing={{}: (2, {})} | custom-call | flops 12884901888 | bytes 46137344 | tf_op jit(solution)/shard_map/pallas_call | solution.py:111
  (20 shorter events, 0.9 us)
Async XLA Ops:
  54.0 156.0 %collective-permute-start = (bf16[64,3,128,128]{2,3,0,1:T(8,128)(2,1)}, bf16[64,3,128,128]{2,3,0,1:T(8,128)(2,1)}, u32[]{:S(2)}, u32[]{:S(2)}) collective-permute-start(bf16[64,3,128,128]{2,3,0,1:T(8,128)(2,1)} %copy.53), channel_id=1, source_target_pairs={{2,0},{4,2},{6,4},{8,6},{10,8},{12,10},{14,12},{3,1},{5,3},{7,5},{... | collective-permute-start | bytes 18874376 | tf_op jit(solution)/shard_map/ppermute | solution.py:17
  87.9 5.7 %copy-start = (f32[4,16384]{1,0:T(4,128)S(1)}, f32[4,16384]{1,0:T(4,128)}, u32[]{:S(2)}) copy-start(f32[4,16384]{1,0:T(4,128)} %param.4) | copy-start | bytes 786436
  87.9 7.2 %copy-start.1 = (s32[64]{0:T(128)S(1)}, s32[64]{0:T(128)}, u32[]{:S(2)}) copy-start(s32[64]{0:T(128)} %param.5) | copy-start | bytes 772
  110.9 173.2 %all-to-all-start.1 = ((bf16[2,64,64,128]{3,2,0,1:T(8,128)(2,1)}), bf16[2,64,64,128]{3,2,0,1:T(8,128)(2,1)S(1)}, u32[]{:S(2)}, u32[]{:S(2)}) async-start(bf16[2,64,64,128]{3,2,0,1:T(8,128)(2,1)} %copy.39), calls=%async_computation.1 | async-start | bytes 4194304 | tf_op jit(solution)/shard_map/all_to_all | solution.py:156
  284.1 84.8 %all-to-all-start = ((bf16[2,64,192,128]{3,2,0,1:T(8,128)(2,1)}), bf16[2,64,192,128]{3,2,0,1:T(8,128)(2,1)}, u32[]{:S(2)}, u32[]{:S(2)}) async-start(bf16[2,64,192,128]{3,2,0,1:T(8,128)(2,1)} %copy.35), calls=%async_computation | async-start | bytes 12582912 | tf_op jit(solution)/shard_map/all_to_all | solution.py:156
  295.7 79.2 %all-gather.5.cloned.1.call-start = ((), (), s32[]{:S(2)}) async-start(), calls=%async_computation.3 | async-start | bytes 6291456 | tf_op jit(solution)/shard_map/all_gather | solution.py:158
  297.4 113.3 %all-gather.3.cloned.1.call-start = ((), (), s32[]{:S(2)}) async-start(), calls=%async_computation.2 | async-start | bytes 18874368 | tf_op jit(solution)/shard_map/all_gather | solution.py:158
Sparse Core Ops, SparseCore 0:
  298.2 20.3 all-gather.4
  375.0 35.5 all-gather.2
